TPU v7x, 256 devices: a whole 4x4x8 slice. The times are simulated.
256 devices in a mesh: kv: 32 (over z, y), tp: 8 (over x, core).
Axes of the slice: x: 4, y: 4, z: 8, core: 2. Of those that a mesh axis runs over, the one named last changes fastest.
Arguments:
- queries: bfloat16 [8, 4, 128, 128], P(None, None, 'tp'), may hold values from -30 to 30
- cache_keys: bfloat16 [8, 8192, 8, 128], P(None, 'kv', 'tp'), may hold values from -4 to 4
- cache_values: bfloat16 [8, 8192, 8, 128], P(None, 'kv', 'tp'), may hold values from -6 to 6
- new_keys: bfloat16 [8, 4, 8, 128], P(None, None, 'tp'), may hold values from -6 to 6
- new_values: bfloat16 [8, 4, 8, 128], P(None, None, 'tp'), may hold values from -6 to 6
- lengths: int32 [8], replicated, may hold values from 512 to 8192
- residual: bfloat16 [32, 16384], P(None, 'kv'), may hold values from -4 to 4
- out_weight: bfloat16 [16384, 16384], P('tp', 'kv'), may hold values from -0.1875 to 0.1875
- norm_gain: bfloat16 [16384], P('kv'), may hold values from 0.099609375 to 1.8984375
- gate_weight: bfloat16 [16384, 26624], P('kv', 'tp'), may hold values from -0.046875 to 0.046875
- up_weight: bfloat16 [16384, 26624], P('kv', 'tp'), may hold values from -0.046875 to 0.046875
- down_weight: bfloat16 [26624, 16384], P('tp', 'kv'), may hold values from -0.0546875 to 0.0546875
Outputs:
- after_attention: bfloat16 [32, 16384], P(None, 'kv')
- layer_out: bfloat16 [32, 16384], P('tp', 'kv')
All inputs are finite; a program needn't handle non-finite values.
Results may differ from a plain program's by a relative error of at most 0.019.
Values may be sent and summed in bfloat16 or wider, within the bound.
A program may use at most 64 MiB of HBM per device.

v0:
```python
import math

import jax
import jax.numpy as jnp
from jax import lax
from jax.sharding import PartitionSpec as P


def turned_gather(arrays, axis, dims):
    turned = [jnp.moveaxis(a, dim, 0) for a, dim in zip(arrays, dims)]
    both = jnp.concatenate([t.reshape(len(t), -1) for t in turned], axis=1)
    result, at, done = (lax.all_gather(both, axis, axis=0, tiled=True), 0, [])
    for t, dim in zip(turned, dims):
        piece = result[:, at : at + t[0].size].reshape(-1, *t.shape[1:])
        done.append(jnp.moveaxis(piece, 0, dim))
        at += t[0].size
    return tuple(done)


def sent_to_all(array, axis):
    copies = jnp.broadcast_to(array, (lax.axis_size(axis), *array.shape))
    return lax.all_to_all(copies, axis, split_axis=0, concat_axis=0, tiled=True)


def of_everyone(array, axis):
    everything = sent_to_all(array, axis)
    return jnp.sum(everything, axis=0)


def split_up(array, dim, peers):
    before, after = (array.shape[:dim], array.shape[dim + 1 :])
    return jnp.moveaxis(array.reshape(*before, peers, -1, *after), dim, 0)


def summed_on_arrival(array, axis, dim):
    peers = lax.axis_size(axis)
    tiles = lax.all_to_all(split_up(array, dim, peers), axis, 0, 0, tiled=True)
    return jnp.sum(tiles, axis=0)


def side_by_side(arrays, axis, dim, along):
    widths = [a.shape[along] for a in arrays]
    both = jnp.concatenate(arrays, axis=along)
    result = summed_on_arrival(both, axis, dim)
    return tuple(jnp.split(result, [sum(widths[:k]) for k in range(1, len(widths))], axis=along))


def laid_out(tiles, dim):
    dims = list(tiles.shape[1:])
    dims[dim] *= tiles.shape[0]
    return jnp.moveaxis(tiles, 0, dim).reshape(dims)


def collect(array, axis, dim):
    return laid_out(sent_to_all(array, axis), dim)


def fold_sources(received):
    source_max, source_total, source_sum = received
    row_max = jnp.max(source_max, axis=0)
    factor = jnp.exp(source_max - row_max[None])
    return (
        row_max,
        jnp.sum(source_total * factor, axis=0),
        jnp.sum(source_sum * factor[..., None], axis=0),
    )


def local(
    queries,
    cache_keys,
    cache_values,
    new_keys,
    new_values,
    lengths,
    residual,
    out_weight,
    norm_gain,
    gate_weight,
    up_weight,
    down_weight,
):
    seq_count, step_count, heads_local, head_dim = queries.shape
    ctx_local = cache_keys.shape[1]
    kv_local = cache_keys.shape[2]
    group_size = heads_local // kv_local
    scaling = 1.0 / math.sqrt(head_dim)
    grouped = queries.reshape(seq_count, step_count, kv_local, group_size, head_dim)
    scores = (
        jnp.einsum("stgjd,scgd->sgjtc", grouped, cache_keys, preferred_element_type=jnp.float32)
        * scaling
    )
    position = lax.axis_index("kv") * ctx_local + lax.iota(jnp.int32, ctx_local)
    in_range = (position[None, :] < lengths[:, None])[:, None, None, None, :]
    masked = jnp.where(in_range, scores, -1e30)
    local_max = jnp.max(masked, axis=-1)
    weights = jnp.where(in_range, jnp.exp(masked - local_max[..., None]), 0.0)
    local_total = jnp.sum(weights, axis=-1)
    local_sum = jnp.einsum(
        "sgjtc,scgd->sgjtd",
        weights.astype(jnp.bfloat16),
        cache_values,
        preferred_element_type=jnp.float32,
    )
    pieces = lax.axis_size("kv")
    row_max, row_total, row_sum = fold_sources(
        (
            lax.all_to_all(
                local_max.reshape(pieces, -1), "kv", split_axis=0, concat_axis=0, tiled=True
            ),
            lax.all_to_all(
                local_total.reshape(pieces, -1), "kv", split_axis=0, concat_axis=0, tiled=True
            ),
            lax.all_to_all(
                local_sum.reshape(pieces, -1, head_dim),
                "kv",
                split_axis=0,
                concat_axis=0,
                tiled=True,
            ),
        )
    )
    gathered_max, gathered_total, gathered_sum = turned_gather(
        (row_max, row_total, row_sum), "kv", (0, 0, 0)
    )
    cache_max = gathered_max.reshape(local_max.shape)
    cache_total = gathered_total.reshape(local_total.shape)
    cache_sum = gathered_sum.reshape(local_sum.shape)
    fresh_scores = (
        jnp.einsum("stgjd,sugd->sgjtu", grouped, new_keys, preferred_element_type=jnp.float32)
        * scaling
    )
    causal = lax.iota(jnp.int32, step_count)[:, None] >= lax.iota(jnp.int32, step_count)[None, :]
    fresh_scores = jnp.where(causal, fresh_scores, -1e30)
    row_top = jnp.maximum(cache_max, jnp.max(fresh_scores, axis=-1))
    carried = jnp.exp(cache_max - row_top)
    fresh_weights = jnp.where(causal, jnp.exp(fresh_scores - row_top[..., None]), 0.0)
    denominator = cache_total * carried + jnp.sum(fresh_weights, axis=-1)
    numerator = cache_sum * carried[..., None] + jnp.einsum(
        "sgjtu,sugd->sgjtd",
        fresh_weights.astype(jnp.bfloat16),
        new_values,
        preferred_element_type=jnp.float32,
    )
    attended = (
        (numerator / denominator[..., None])
        .transpose(0, 3, 1, 2, 4)
        .reshape(seq_count * step_count, heads_local * head_dim)
        .astype(jnp.bfloat16)
    )
    projected = of_everyone(jnp.dot(attended, out_weight, preferred_element_type=jnp.float32), "tp")
    after_attention = (residual.astype(jnp.float32) + projected).astype(jnp.bfloat16)
    wide_rows = after_attention.astype(jnp.float32)
    model_width = norm_gain.shape[0] * lax.axis_size("kv")
    squares = of_everyone(jnp.sum(wide_rows * wide_rows, axis=1), "kv")
    inverse = lax.rsqrt(squares / model_width + 1e-05)
    normed = (wide_rows * norm_gain.astype(jnp.float32)[None, :] * inverse[:, None]).astype(
        jnp.bfloat16
    )
    gate_part = jnp.dot(normed, gate_weight, preferred_element_type=jnp.float32)
    up_part = jnp.dot(normed, up_weight, preferred_element_type=jnp.float32)
    gate_share, up_share = side_by_side((gate_part, up_part), "kv", 1, 0)
    hidden = collect((jax.nn.silu(gate_share) * up_share).astype(jnp.bfloat16), "kv", 1)
    rows_own = hidden.shape[0] // lax.axis_size("tp")
    own_sums = summed_on_arrival(
        jnp.dot(hidden, down_weight, preferred_element_type=jnp.float32), "tp", 0
    )
    residual_rows = lax.dynamic_slice_in_dim(
        wide_rows, lax.axis_index("tp") * rows_own, rows_own, 0
    )
    return (after_attention, (residual_rows + own_sums).astype(jnp.bfloat16))


def solution(mesh):
    return jax.shard_map(
        local,
        mesh=mesh,
        in_specs=(
            P(None, None, "tp", None),
            P(None, "kv", "tp", None),
            P(None, "kv", "tp", None),
            P(None, None, "tp", None),
            P(None, None, "tp", None),
            P(),
            P(None, "kv"),
            P("tp", "kv"),
            P("kv"),
            P("kv", "tp"),
            P("kv", "tp"),
            P("tp", "kv"),
        ),
        out_specs=(P(None, "kv"), P("tp", "kv")),
        check_vma=False,
    )
```

profile of v0, /device:TPU:1, one launch (start us, length us, event | category | flops | bytes accessed | tf_op | source)
XLA Modules:
  0.0 220.3 jit_solution(5743829172851007249)
XLA Ops:
  2.2 2.2 fusion.37
  5.1 1.5 all_to_all.35
  6.6 12.2 %all-to-all-start = ((f32[32,1,16]{2,1,0:T(1,128)}), f32[32,1,16]{2,1,0:T(1,128)}, u32[]{:S(2)}, u32[]{:S(2)}) async-start(f32[32,1,16]{2,1,0:T(1,128)} %bitcast.93), calls=%async_computation | async-start | bytes 32768 | tf_op jit(solution)/shard_map/all_to_all | solution.py:108
  18.8 1.9 fusion.13
  22.1 1.5 all_to_all.37
  23.7 3.5 %all-to-all-done = f32[32,1,16]{2,1,0:T(1,128)} async-done(((f32[32,1,16]{2,1,0:T(1,128)}), f32[32,1,16]{2,1,0:T(1,128)}, u32[]{:S(2)}, u32[]{:S(2)}) %all-to-all-start) | async-done | bytes 2080 | tf_op jit(solution)/shard_map/all_to_all | solution.py:108
  27.2 5.7 %all-to-all-start.1 = ((f32[32,1,16]{2,1,0:T(1,128)}), f32[32,1,16]{2,1,0:T(1,128)}, u32[]{:S(2)}, u32[]{:S(2)}) async-start(f32[32,1,16]{2,1,0:T(1,128)} %bitcast.92), calls=%async_computation.1 | async-start | bytes 32768 | tf_op jit(solution)/shard_map/all_to_all | solution.py:111
  35.2 6.2 %all-to-all-done.1 = f32[32,1,16]{2,1,0:T(1,128)} async-done(((f32[32,1,16]{2,1,0:T(1,128)}), f32[32,1,16]{2,1,0:T(1,128)}, u32[]{:S(2)}, u32[]{:S(2)}) %all-to-all-start.1) | async-done | bytes 2080 | tf_op jit(solution)/shard_map/all_to_all | solution.py:111
  41.5 4.6 %all-to-all-start.2 = ((f32[32,16,128]{2,1,0:T(8,128)}), f32[32,16,128]{2,1,0:T(8,128)}, u32[]{:S(2)}, u32[]{:S(2)}) async-start(f32[32,16,128]{2,1,0:T(8,128)} %bitcast.86), calls=%async_computation.2 | async-start | bytes 524288 | tf_op jit(solution)/shard_map/all_to_all | solution.py:114
  46.6 1.7 fusion.38
  50.0 6.6 %all-to-all-done.2 = f32[32,16,128]{2,1,0:T(8,128)} async-done(((f32[32,16,128]{2,1,0:T(8,128)}), f32[32,16,128]{2,1,0:T(8,128)}, u32[]{:S(2)}, u32[]{:S(2)}) %all-to-all-start.2) | async-done | bytes 262176 | tf_op jit(solution)/shard_map/all_to_all | solution.py:114
  57.8 35.3 %all_gather.3 = f32[512,130]{1,0:T(8,128)S(1)} all-gather(f32[16,130]{1,0:T(8,128)S(1)} %pad_maximum_fusion.1), channel_id=1, replica_groups=mesh['kv'=32,'tp'=8] {'kv'}, dimensions={0}, use_global_device_ids=true | all-gather | bytes 274560 | tf_op jit(solution)/shard_map/all_gather | solution.py:12
  97.1 2.0 fusion.19
  99.2 29.3 %all_to_all.55 = f32[8,32,512]{2,1,0:T(8,128)} all-to-all(f32[8,32,512]{2,1,0:T(8,128)S(1)} %broadcast_in_dim.63), channel_id=1, replica_groups=mesh['kv'=32,'tp'=8] {'tp'}, dimensions={0} | all-to-all | bytes 1048576 | tf_op jit(solution)/shard_map/all_to_all | solution.py:22
  131.0 4.9 %all-to-all-start.4 = ((f32[32,1,32]{2,1,0:T(1,128)}), f32[32,1,32]{2,1,0:T(1,128)S(1)}, u32[]{:S(2)}, u32[]{:S(2)}) async-start(f32[32,1,32]{2,1,0:T(1,128)} %broadcast_in_dim.64), calls=%async_computation.4 | async-start | bytes 32768 | tf_op jit(solution)/shard_map/all_to_all | solution.py:22
  135.9 8.6 %all-to-all-done.4 = f32[32,1,32]{2,1,0:T(1,128)S(1)} async-done(((f32[32,1,32]{2,1,0:T(1,128)}), f32[32,1,32]{2,1,0:T(1,128)S(1)}, u32[]{:S(2)}, u32[]{:S(2)}) %all-to-all-start.4) | async-done | bytes 4128 | tf_op jit(solution)/shard_map/all_to_all | solution.py:22
  148.2 3.4 %reshape.205 = f32[64,32,104]{2,1,0:T(8,128)} reshape(f32[64,3328]{1,0:T(8,128)} %pad_maximum_fusion) | data formatting | bytes 1703936 | tf_op jit(solution)/shard_map/reshape | solution.py:32
  151.6 1.8 copy.78
  153.4 28.8 %all_to_all.56 = f32[32,64,104]{2,1,0:T(8,128)} all-to-all(f32[32,64,104]{2,1,0:T(8,128)S(1)} %bitcast.85), channel_id=1, replica_groups=mesh['kv'=32,'tp'=8] {'kv'}, dimensions={0} | all-to-all | bytes 1703936 | tf_op jit(solution)/shard_map/all_to_all | solution.py:37
  183.6 17.1 %all_to_all.57 = bf16[32,32,104]{2,1,0:T(8,128)(2,1)S(1)} all-to-all(bf16[32,32,104]{2,1,0:T(8,128)(2,1)S(1)} %broadcast_in_dim.65), channel_id=1, replica_groups=mesh['kv'=32,'tp'=8] {'kv'}, dimensions={0} | all-to-all | bytes 425984 | tf_op jit(solution)/shard_map/all_to_all | solution.py:22
  201.5 2.1 dot_general.33
  203.6 3.3 %fusion = f32[8,4,512]{2,1,0:T(4,128)} fusion(bf16[8,4,3328]{2,1,0:T(4,128)(2,1)} %dot_general.33, bf16[3328,512]{1,0:T(8,128)(2,1)} %param.23), kind=kOutput, calls=%fused_computation | convolution fusion | flops 109051904 | bytes 3686400 | tf_op jit(solution)/shard_map/dot_general | solution.py:166
  207.0 7.1 %all-to-all-start.7 = ((f32[8,4,512]{2,1,0:T(4,128)}), f32[8,4,512]{2,1,0:T(4,128)S(1)}, u32[]{:S(2)}, u32[]{:S(2)}) async-start(f32[8,4,512]{2,1,0:T(4,128)} %fusion), calls=%async_computation.7 | async-start | bytes 131072 | tf_op jit(solution)/shard_map/all_to_all | solution.py:37
  214.1 4.9 %all-to-all-done.7 = f32[8,4,512]{2,1,0:T(4,128)S(1)} async-done(((f32[8,4,512]{2,1,0:T(4,128)}), f32[8,4,512]{2,1,0:T(4,128)S(1)}, u32[]{:S(2)}, u32[]{:S(2)}) %all-to-all-start.7) | async-done | bytes 65568 | tf_op jit(solution)/shard_map/all_to_all | solution.py:37
  (56 shorter events, 23.0 us)
Async XLA Ops:
  0.6 143.9 %copy-start = (bf16[512,3328]{1,0:T(8,128)(2,1)S(1)}, bf16[512,3328]{1,0:T(8,128)(2,1)}, u32[]{:S(2)}) copy-start(bf16[512,3328]{1,0:T(8,128)(2,1)} %param.22) | copy-start | bytes 10223620
  0.6 45.9 %copy-start.3 = (bf16[8,4,16,128]{3,2,1,0:T(8,128)(2,1)S(1)}, bf16[8,4,16,128]{3,2,1,0:T(8,128)(2,1)}, u32[]{:S(2)}) copy-start(bf16[8,4,16,128]{3,2,1,0:T(8,128)(2,1)} %param.12) | copy-start | bytes 393220
  1.6 0.6 copy-start.4
  6.6 20.6 %all-to-all-start = ((f32[32,1,16]{2,1,0:T(1,128)}), f32[32,1,16]{2,1,0:T(1,128)}, u32[]{:S(2)}, u32[]{:S(2)}) async-start(f32[32,1,16]{2,1,0:T(1,128)} %bitcast.93), calls=%async_computation | async-start | bytes 32768 | tf_op jit(solution)/shard_map/all_to_all | solution.py:108
  27.2 14.3 %all-to-all-start.1 = ((f32[32,1,16]{2,1,0:T(1,128)}), f32[32,1,16]{2,1,0:T(1,128)}, u32[]{:S(2)}, u32[]{:S(2)}) async-start(f32[32,1,16]{2,1,0:T(1,128)} %bitcast.92), calls=%async_computation.1 | async-start | bytes 32768 | tf_op jit(solution)/shard_map/all_to_all | solution.py:111
  41.5 15.2 %all-to-all-start.2 = ((f32[32,16,128]{2,1,0:T(8,128)}), f32[32,16,128]{2,1,0:T(8,128)}, u32[]{:S(2)}, u32[]{:S(2)}) async-start(f32[32,16,128]{2,1,0:T(8,128)} %bitcast.86), calls=%async_computation.2 | async-start | bytes 524288 | tf_op jit(solution)/shard_map/all_to_all | solution.py:114
  46.1 0.5 copy-start.6
  94.2 35.3 %copy-start.5 = (bf16[32,512]{1,0:T(8,128)(2,1)S(1)}, bf16[32,512]{1,0:T(8,128)(2,1)}, u32[]{:S(2)}) copy-start(bf16[32,512]{1,0:T(8,128)(2,1)} %param.18) | copy-start | bytes 98308
  94.7 41.1 %copy-start.7 = (bf16[512]{0:T(512)(128)(2,1)S(1)}, bf16[512]{0:T(512)(128)(2,1)}, u32[]{:S(2)}) copy-start(bf16[512]{0:T(512)(128)(2,1)} %param.20) | copy-start | bytes 3076
  130.2 16.9 %copy-start.2 = (bf16[32,512]{1,0:T(8,128)(2,1)}, bf16[32,512]{1,0:T(8,128)(2,1)S(1)}, u32[]{:S(2)}) copy-start(bf16[32,512]{1,0:T(8,128)(2,1)S(1)} %get-tuple-element.5) | copy-start | bytes 98308
  131.0 13.5 %all-to-all-start.4 = ((f32[32,1,32]{2,1,0:T(1,128)}), f32[32,1,32]{2,1,0:T(1,128)S(1)}, u32[]{:S(2)}, u32[]{:S(2)}) async-start(f32[32,1,32]{2,1,0:T(1,128)} %broadcast_in_dim.64), calls=%async_computation.4 | async-start | bytes 32768 | tf_op jit(solution)/shard_map/all_to_all | solution.py:22
  144.5 2.0 copy-start.1
  207.0 12.0 %all-to-all-start.7 = ((f32[8,4,512]{2,1,0:T(4,128)}), f32[8,4,512]{2,1,0:T(4,128)S(1)}, u32[]{:S(2)}, u32[]{:S(2)}) async-start(f32[8,4,512]{2,1,0:T(4,128)} %fusion), calls=%async_computation.7 | async-start | bytes 131072 | tf_op jit(solution)/shard_map/all_to_all | solution.py:37
where the time goes:
time: 222 us; the launch traced here: 220 us
  blocking collectives  110 us (50%)
  starting transfers between devices  34.5 us (16%)
  waiting for transfers between devices  29.8 us (13%)
  local copies, waits for them, and re-layouts  19 us (9%)
  matrix products  13.6 us (6%)
  other arithmetic  12.1 us (5%)
    all_to_all x2, blocking collectives, sent_to_all(): return lax.all_to_all(copies, axis, split_axis=0, concat_axis=0, tiled=True)  46.4 us
    all_gather x1, blocking collectives, turned_gather(): result, at, done = (lax.all_gather(both, axis, axis=0, tiled=True), 0, [])  35.3 us
    all_to_all x1, blocking collectives, summed_on_arrival(): tiles = lax.all_to_all(split_up(array, dim, peers), axis, 0, 0, tiled=True)  28.8 us
    all_to_all x1, starting transfers between devices, local(): lax.all_to_all(local_max.reshape(pieces, -1), 'kv', split_axis=0, concat_...  12.2 us
    all_to_all x1, waiting for transfers between devices, sent_to_all(): return lax.all_to_all(copies, axis, split_axis=0, concat_axis=0, tiled=True)  8.6 us
    all_to_all x1, starting transfers between devices, summed_on_arrival(): tiles = lax.all_to_all(split_up(array, dim, peers), axis, 0, 0, tiled=True)  7.12 us
    all_to_all x1, waiting for transfers between devices, local(): lax.all_to_all(local_sum.reshape(pieces, -1, head_dim), 'kv', split_axis=...  6.58 us
    all_to_all x1, waiting for transfers between devices, local(): lax.all_to_all(local_total.reshape(pieces, -1), 'kv', split_axis=0, conca...  6.2 us
  transfers between devices with their start and end apart: 5, of which 5 were waited for; matrix products, arithmetic and copies ran while one was open for 4% of the time, Pallas kernels for 0%

commit v1 on v0

v1 whole, which is shorter than its diff:
```python
import math

import jax
import jax.numpy as jnp
from jax import lax
from jax.experimental import pallas as pl
from jax.experimental.pallas import tpu as pltpu
from jax.sharding import PartitionSpec as P

F32, BF16 = jnp.float32, jnp.bfloat16
MESH = pl.DeviceIdType.MESH
Z, Y, TP = 8, 4, 8
KV = Z * Y
SEQS, STEPS, HEADS, HD = 8, 4, 16, 128
CTX = 256
COLS = 512
MODEL = 16384
FF = 3328
WIDTH = (3, 3, 3, 3, 3, 3, 4, 4)
START = tuple(sum(WIDTH[:c]) * 128 for c in range(Z))
SCALE = 1.0 / math.sqrt(HD)
LOW = -1e30


def drain(ref, sem):
    pltpu.make_async_copy(ref, ref, sem).wait()


def kernel(
    lengths,
    q_in, k_in, v_in, nk_in, nv_in, res_in, wo_in, gain_in, wg_in, wu_in, wd_in,
    after_out, layer_out,
    qv, kb, vb, nkb, nvb, resb, wo, gainb, wg, wu, wd,
    obuf, sbuf, ra, rs, tb, gb, gf, pr, aft,
    sqb, sqr, sqz, yb, yr, zs, zr, hr, fs, fr,
    load_sem, a_send, a_recv, b_send, b_recv, c_send, c_recv,
    y_send, y_recv, sq_send, sq_recv, z_send, z_recv,
    hz_send, hz_recv, hy_send, hy_recv, f_send, f_recv,
):
    kv, tp = lax.axis_index("kv"), lax.axis_index("tp")
    z, y = kv // Y, kv % Y
    x, core = tp // 2, tp % 2

    pairs = (
        (q_in, qv), (k_in, kb), (v_in, vb), (nk_in, nkb), (nv_in, nvb), (res_in, resb), (gain_in, gainb),
        (wo_in, wo), (wg_in, wg), (wu_in, wu), (wd_in, wd),
    )
    loads = [pltpu.make_async_copy(a, b, load_sem.at[i]) for i, (a, b) in enumerate(pairs)]
    for copy in loads:
        copy.start()
    l_q, l_k, l_v, l_nk, l_nv, l_res, l_gain, l_wo, l_wg, l_wu, l_wd = loads

    def send(src, dst, send_sem, recv_sem, to):
        pltpu.make_async_remote_copy(
            src_ref=src, dst_ref=dst, send_sem=send_sem, recv_sem=recv_sem, device_id=to, device_id_type=MESH
        ).start()

    barrier = pltpu.get_barrier_semaphore()

    @pl.loop(1, KV)
    def _(i):
        pl.semaphore_signal(barrier, inc=1, device_id=(lax.rem(kv + i, KV), tp), device_id_type=MESH)

    @pl.loop(1, TP)
    def _(i):
        pl.semaphore_signal(barrier, inc=1, device_id=(kv, lax.rem(tp + i, TP)), device_id_type=MESH)

    l_q.wait()
    l_k.wait()
    l_v.wait()
    position = lax.broadcasted_iota(jnp.int32, (STEPS * HEADS, CTX), 1) + kv * CTX
    lane = lax.broadcasted_iota(jnp.int32, (128, 128), 1)
    stats = jnp.zeros((128, 128), F32)
    for s in range(SEQS):
        rows = qv[s * STEPS : (s + 1) * STEPS].reshape(STEPS * HEADS, HD)
        scores = lax.dot_general(rows, kb[s], (((1,), (1,)), ((), ())), preferred_element_type=F32) * SCALE
        inside = position < lengths[s]
        scores = jnp.where(inside, scores, LOW)
        top = jnp.max(scores, axis=1, keepdims=True)
        weights = jnp.where(inside, jnp.exp(scores - top), 0.0)
        total = jnp.sum(weights, axis=1, keepdims=True)
        sums = jnp.dot(weights.astype(BF16), vb[s], preferred_element_type=F32)
        obuf[s * STEPS : (s + 1) * STEPS] = sums.reshape(STEPS, HEADS, HD).astype(BF16)
        stats = jnp.where(lane == s, jnp.concatenate([top, total], axis=0), stats)
    turned = stats.T
    for s in range(SEQS):
        sbuf[s] = turned[s : s + 1]

    pl.semaphore_wait(barrier, KV - 1 + TP - 1)

    @pl.loop(1, KV)
    def _(i):
        to = lax.rem(kv + i, KV)
        send(sbuf.at[to // Y], rs.at[KV - 1 - i], a_send.at[0], a_recv.at[0], (to, tp))
        send(obuf.at[to], ra.at[KV - 1 - i], a_send.at[1], a_recv.at[1], (to, tp))

    l_nk.wait()
    l_nv.wait()
    own_q = qv[kv].astype(F32)
    fresh_k, fresh_v = nkb[z].astype(F32), nvb[z].astype(F32)
    fresh = []
    for u in range(STEPS):
        score = jnp.sum(own_q * fresh_k[u : u + 1], axis=1, keepdims=True) * SCALE
        fresh.append(jnp.where(u <= y, score, LOW))
    rs[KV - 1] = sbuf[z]
    drain(rs.at[0 : KV - 1], a_recv.at[0])
    tb[:, 0:KV] = rs[...].reshape(KV, 128).T
    tops = tb[pl.ds(pl.multiple_of(y * HEADS, HEADS), HEADS), 0:KV]
    totals = tb[pl.ds(pl.multiple_of(64 + y * HEADS, HEADS), HEADS), 0:KV]
    row_max = jnp.max(tops, axis=1, keepdims=True)
    for score in fresh:
        row_max = jnp.maximum(row_max, score)
    factor = jnp.exp(tops - row_max)
    denominator = jnp.sum(factor * totals, axis=1, keepdims=True)
    numerator = factor[:, KV - 1 : KV] * obuf[kv].astype(F32)
    for u in range(STEPS):
        weight = jnp.where(u <= y, jnp.exp(fresh[u] - row_max), 0.0)
        denominator += weight
        numerator += weight.astype(BF16).astype(F32) * fresh_v[u : u + 1]
    drain(ra, a_recv.at[1])
    for j in range(KV - 1):
        numerator += factor[:, j : j + 1] * ra[j].astype(F32)
    gb[kv] = (numerator / denominator).astype(BF16)

    @pl.loop(1, KV)
    def _(i):
        to = lax.rem(kv + i, KV)
        send(gb.at[kv], gb.at[kv], b_send, b_recv, (to, tp))

    l_wo.wait()
    l_res.wait()
    l_gain.wait()
    drain(gb.at[0 : KV - 1], b_recv)
    gf[...] = gb[...].astype(F32).reshape(KV * HEADS, HD)
    attended = jnp.concatenate(
        [gf[pl.ds(h, KV, stride=HEADS), :].astype(BF16) for h in range(HEADS)], axis=1
    )
    pr[tp] = jnp.dot(attended, wo[...], preferred_element_type=F32).astype(BF16)

    @pl.loop(1, TP)
    def _(i):
        send(pr.at[tp], pr.at[tp], c_send, c_recv, (kv, lax.rem(tp + i, TP)))

    drain(pr.at[0 : TP - 1], c_recv)
    summed = resb[...].astype(F32)
    for t in range(TP):
        summed += pr[t].astype(F32)
    after = summed.astype(BF16)
    after_out[...] = after
    wide = after.astype(F32)
    aft[...] = wide

    sqb[...] = jnp.broadcast_to(jnp.sum(wide * wide, axis=1, keepdims=True), (KV, 128)).reshape(Y, 8, 128)

    def over_y(body):
        for i in range(1, Y):
            p = lax.rem(y + i, Y)
            body(p, Y - 1 - i, (z * Y + p, tp))

    def over_z(body):
        for i in range(1, Z):
            p = lax.rem(z + i, Z)
            body((p * Y + y, tp))

    over_y(lambda p, slot, to: send(sqb.at[p], sqr.at[slot], sq_send.at[0], sq_recv.at[0], to))
    normed = (wide * gainb[...].astype(F32)).astype(BF16)

    def finish_y(c):
        n = WIDTH[c] * 256
        drain(yr.at[c, :, :, 0:n], y_recv.at[c])
        part = yb[c, y, :, 0:n].astype(F32)
        for i in range(Y - 1):
            part += yr[c, i, :, 0:n].astype(F32)
        zs[c, :, 0:n] = part.astype(BF16)

        @pl.when(z != c)
        def _():
            send(zs.at[c, :, 0:n], zr.at[z, :, 0:n], z_send.at[c], z_recv, (c * Y + y, tp))

    l_wg.wait()
    l_wu.wait()
    lag = 3
    for c in range(Z):
        n, at = WIDTH[c], START[c]
        gate = jnp.dot(normed, wg[:, at : at + n * 128], preferred_element_type=F32)
        up = jnp.dot(normed, wu[:, at : at + n * 128], preferred_element_type=F32)
        for j in range(n):
            for half, value in enumerate((gate, up)):
                tile = value[:, j * 128 : (j + 1) * 128].reshape(Y, 8, 128)
                yb[c, :, :, j * 256 + half * 128 : j * 256 + half * 128 + 128] = tile.astype(BF16)
        over_y(
            lambda p, slot, to: send(
                yb.at[c, p, :, 0 : n * 256], yr.at[c, slot, :, 0 : n * 256], y_send.at[c], y_recv.at[c], to
            )
        )
        if c == lag - 1:
            drain(sqr, sq_recv.at[0])
            sqz[z] = sqb[y] + sqr[0] + sqr[1] + sqr[2]
            over_z(lambda to: send(sqz.at[z], sqz.at[z], sq_send.at[1], sq_recv.at[1], to))
        if c >= lag:
            finish_y(c - lag)
    for c in range(Z - lag, Z):
        finish_y(c)

    zr[z] = zs[z]
    drain(sqz.at[0 : Z - 1], sq_recv.at[1])
    squares = sqz[0]
    for i in range(1, Z):
        squares += sqz[i]
    inverse = lax.rsqrt(squares / MODEL + 1e-05)

    @pl.when(z < 6)
    def _():
        drain(zr.at[0 : Z - 1, :, 0:768], z_recv)

    @pl.when(z >= 6)
    def _():
        drain(zr.at[0 : Z - 1, :, 0:1024], z_recv)

    both = zr[0].astype(F32)
    for i in range(1, Z):
        both += zr[i].astype(F32)
    for j in range(4):
        gate = both[:, j * 256 : j * 256 + 128] * inverse
        up = both[:, j * 256 + 128 : j * 256 + 256] * inverse
        hr[z, y, :, j * 128 : (j + 1) * 128] = (gate / (1.0 + jnp.exp(-gate)) * up).astype(BF16)

    def send_hidden(n):
        own = hr.at[z, y, :, 0:n]
        over_z(lambda to: send(own, own, hz_send, hz_recv.at[z], to))
        over_y(lambda p, slot, to: send(own, own, hy_send.at[z], hy_recv.at[z], to))

    @pl.when(z < 6)
    def _():
        send_hidden(384)

    @pl.when(z >= 6)
    def _():
        send_hidden(512)

    for c in range(Z):
        n = WIDTH[c] * 128

        @pl.when(z != c)
        def _():
            piece = hr.at[c, y, :, 0:n]
            drain(piece, hz_recv.at[c])
            over_y(lambda p, slot, to: send(piece, piece, hy_send.at[c], hy_recv.at[c], to))

    l_wd.wait()
    down = jnp.zeros((KV, COLS), F32)
    for c in range(Z):
        n = WIDTH[c] * 128
        drain(hr.at[c, 0 : Y - 1, :, 0:n], hy_recv.at[c])
        hidden = hr[c, :, :, 0:n].astype(F32).reshape(KV, n).astype(BF16)
        down += jnp.dot(hidden, wd[START[c] : START[c] + n, :], preferred_element_type=F32)
    fs[...] = down.reshape(4, 8, COLS).astype(BF16)

    @pl.loop(1, TP)
    def _(i):
        to = lax.rem(tp + i, TP)
        send(fs.at[to // 2], fr.at[TP - 1 - i], f_send, f_recv, (kv, to))

    rows = aft[pl.ds(pl.multiple_of(x * 8, 8), 8), :] + fs[x].astype(F32)
    drain(fr, f_recv)
    for i in range(TP - 1):
        rows += fr[i].astype(F32)
    layer_out[...] = jnp.where(core == 0, rows[0:4], rows[4:8]).astype(BF16)

    drain(rs.at[0 : KV - 1], a_send.at[0])
    drain(ra, a_send.at[1])
    drain(gb.at[0 : KV - 1], b_send)
    drain(pr.at[0 : TP - 1], c_send)
    drain(sqr, sq_send.at[0])
    drain(sqz.at[0 : Z - 1], sq_send.at[1])
    for c in range(Z):
        n = WIDTH[c] * 128
        drain(yr.at[c, :, :, 0 : 2 * n], y_send.at[c])
        drain(hr.at[c, 0 : Y - 1, :, 0:n], hy_send.at[c])

        @pl.when(z != c)
        def _():
            drain(zs.at[c, :, 0 : 2 * n], z_send.at[c])

    @pl.when(z < 6)
    def _():
        drain(hr.at[0 : Z - 1, 0, :, 0:384], hz_send)

    @pl.when(z >= 6)
    def _():
        drain(hr.at[0 : Z - 1, 0, :, 0:512], hz_send)

    drain(fr, f_send)


def local(queries, cache_keys, cache_values, new_keys, new_values, lengths, residual, out_weight, norm_gain,
          gate_weight, up_weight, down_weight):
    hbm = pl.BlockSpec(memory_space=pl.ANY)
    vmem = pl.BlockSpec(memory_space=pltpu.VMEM)
    dma = pltpu.SemaphoreType.DMA
    return pl.pallas_call(
        kernel,
        out_shape=(jax.ShapeDtypeStruct((KV, COLS), BF16), jax.ShapeDtypeStruct((4, COLS), BF16)),
        in_specs=[pl.BlockSpec(memory_space=pltpu.SMEM)] + [hbm] * 11,
        out_specs=(vmem, vmem),
        scratch_shapes=[
            pltpu.VMEM((KV, HEADS, HD), BF16),
            pltpu.VMEM((SEQS, CTX, HD), BF16),
            pltpu.VMEM((SEQS, CTX, HD), BF16),
            pltpu.VMEM((SEQS, STEPS, HD), BF16),
            pltpu.VMEM((SEQS, STEPS, HD), BF16),
            pltpu.VMEM((KV, COLS), BF16),
            pltpu.VMEM((HEADS * HD, COLS), BF16),
            pltpu.VMEM((1, COLS), F32),
            pltpu.VMEM((COLS, FF), BF16),
            pltpu.VMEM((COLS, FF), BF16),
            pltpu.VMEM((FF, COLS), BF16),
            pltpu.VMEM((KV, HEADS, HD), BF16),
            pltpu.VMEM((SEQS, 1, 128), F32),
            pltpu.VMEM((KV - 1, HEADS, HD), BF16),
            pltpu.VMEM((KV, 1, 128), F32),
            pltpu.VMEM((128, 128), F32),
            pltpu.VMEM((KV, HEADS, HD), BF16),
            pltpu.VMEM((KV * HEADS, HD), F32),
            pltpu.VMEM((TP, KV, COLS), BF16),
            pltpu.VMEM((KV, COLS), F32),
            pltpu.VMEM((Y, 8, 128), F32),
            pltpu.VMEM((Y - 1, 8, 128), F32),
            pltpu.VMEM((Z, 8, 128), F32),
            pltpu.VMEM((Z, Y, 8, 1024), BF16),
            pltpu.VMEM((Z, Y - 1, 8, 1024), BF16),
            pltpu.VMEM((Z, 8, 1024), BF16),
            pltpu.VMEM((Z, 8, 1024), BF16),
            pltpu.VMEM((Z, Y, 8, 512), BF16),
            pltpu.VMEM((4, 8, COLS), BF16),
            pltpu.VMEM((TP - 1, 8, COLS), BF16),
            dma((11,)), dma((2,)), dma((2,)), dma, dma, dma, dma,
            dma((Z,)), dma((Z,)), dma((2,)), dma((2,)), dma((Z,)), dma,
            dma, dma((Z,)), dma((Z,)), dma((Z,)), dma, dma,
        ],
        compiler_params=pltpu.CompilerParams(
            collective_id=0, has_side_effects=True, vmem_limit_bytes=60 * 1024 * 1024
        ),
    )(
        lengths,
        queries.reshape(KV, HEADS, HD),
        cache_keys.reshape(SEQS, CTX, HD),
        cache_values.reshape(SEQS, CTX, HD),
        new_keys.reshape(SEQS, STEPS, HD),
        new_values.reshape(SEQS, STEPS, HD),
        residual,
        out_weight,
        norm_gain.astype(F32).reshape(1, COLS),
        gate_weight,
        up_weight,
        down_weight,
    )


def solution(mesh):
    return jax.shard_map(
        local,
        mesh=mesh,
        in_specs=(
            P(None, None, "tp", None),
            P(None, "kv", "tp", None),
            P(None, "kv", "tp", None),
            P(None, None, "tp", None),
            P(None, None, "tp", None),
            P(),
            P(None, "kv"),
            P("tp", "kv"),
            P("kv"),
            P("kv", "tp"),
            P("kv", "tp"),
            P("tp", "kv"),
        ),
        out_specs=(P(None, "kv"), P("tp", "kv")),
        check_vma=False,
    )
```

time: 222 us -> 63.8 us (0.29)
  blocking collectives: 110 us -> 0 us
  Pallas kernels: 0 us -> 59.1 us
  starting transfers between devices: 34.5 us -> 0 us
  waiting for transfers between devices: 29.8 us -> 0 us
  local copies, waits for them, and re-layouts: 19 us -> 2.65 us
  matrix products: 13.6 us -> 0 us
  other arithmetic: 12.1 us -> 1.26 us
    all_to_all x3 -> x0, blocking collectives: 75.1 us -> none  [the longest x2 46.4 us: sent_to_all(): return lax.all_to_all(copies, axis, split_axis=0, concat_axis=0, tiled=True)]
    pallas_call x0 -> x1, Pallas kernels: none -> 59.1 us  [local(): pl.pallas_call(kernel, out_shape=(jax.ShapeDtypeStruct((KV, COLS), BF16),...]
    all_gather x1 -> x0, blocking collectives: 35.3 us -> none  [turned_gather(): result, at, done = (lax.all_gather(both, axis, axis=0, tiled=True), 0, [])]
    all_to_all x5 -> x0, starting transfers between devices: 34.5 us -> none  [the longest x1 12.2 us: local(): lax.all_to_all(local_max.reshape(pieces, -1), 'kv', split_axis=0, concat_...]
    all_to_all x5 -> x0, waiting for transfers between devices: 29.8 us -> none  [the longest x1 8.6 us: sent_to_all(): return lax.all_to_all(copies, axis, split_axis=0, concat_axis=0, tiled=True)]
    dot_general x8 -> x0, matrix products: 13.6 us -> none  [the longest x1 3.35 us: local(): jnp.dot(hidden, down_weight, preferred_element_type=jnp.float32)]
    reduce_sum x9 -> x0, other arithmetic: 7.3 us -> none  [the longest x1 1.93 us: local(): local_total = jnp.sum(weights, axis=-1)]
    reshape x4 -> x0, local copies, waits for them, and re-layouts: 5.41 us -> none  [the longest x2 5.24 us: split_up(): return jnp.moveaxis(array.reshape(*before, peers, -1, *after), dim, 0)]
  transfers between devices with their start and end apart: 5 -> 0, of which waited for: 5 -> 0; matrix products, arithmetic and copies ran while one was open for 4% -> 0% of each run, Pallas kernels for 0% -> 0%
where the time goes in v1:
time: 63.8 us; the launch traced here: 63.6 us
  Pallas kernels  59.1 us (93%)
  local copies, waits for them, and re-layouts  2.65 us (4%)
  other arithmetic  1.26 us (2%)
  between operations  0.64 us (1%)
    pallas_call x1, Pallas kernels, local(): pl.pallas_call(kernel, out_shape=(jax.ShapeDtypeStruct((KV, COLS), BF16),...  59.1 us
    unnamed x2, local copies, waits for them, and re-layouts  2.65 us

profile of v1, /device:TPU:1, one launch (start us, length us, event | category | flops | bytes accessed | tf_op | source)
XLA Modules:
  0.0 63.6 jit_solution(6407244057837792351)
XLA Ops:
  0.6 1.3 %reshape.31 = f32[512]{0:T(512)} convert(bf16[512]{0:T(512)(128)(2,1)} %param.20) | non-fusion elementwise | flops 512 | bytes 3072 | tf_op jit(solution)/shard_map/reshape | solution.py:353
  1.9 59.1 %shard_map.131 = (bf16[32,512]{1,0:T(8,128)(2,1)}, bf16[4,512]{1,0:T(4,128)(2,1)}) custom-call(s32[8]{0:T(128)} %lengths.1, bf16[32,16,128]{2,1,0:T(8,128)(2,1)} %bitcast.8, bf16[8,256,128]{2,1,0:T(8,128)(2,1)} %bitcast.6, bf16[8,256,128]{2,1,0:T(8,128)(2,1)} %bitcast.7, bf16[8,4,128]{2,1,0:T(4,128)(2,1)} %bitcast.10, bf16[8,4,128]{2,1,0:T(4,128)(2,1)} %bitcast.11, ...), custom_call_target="tpu_custom_call" | custom-call | tf_op jit(solution)/shard_map/pallas_call | solution.py:301
  61.0 1.4 %copy.16 = bf16[32,512]{1,0:T(8,128)(2,1)} copy(bf16[32,512]{1,0:T(8,128)(2,1)} %get-tuple-element.4) | data formatting | bytes 65536
  62.4 1.3 %copy.17 = bf16[4,512]{1,0:T(4,128)(2,1)} copy(bf16[4,512]{1,0:T(4,128)(2,1)} %get-tuple-element.5) | data formatting | bytes 8192

commit v2 on v1

v2 whole, which is shorter than its diff:
```python
import math

import jax
import jax.numpy as jnp
from jax import lax
from jax.experimental import pallas as pl
from jax.experimental.pallas import tpu as pltpu
from jax.sharding import PartitionSpec as P

F32, BF16 = jnp.float32, jnp.bfloat16
MESH = pl.DeviceIdType.MESH
Z, Y, TP = 8, 4, 8
KV = Z * Y
SEQS, STEPS, HEADS, HD = 8, 4, 16, 128
CTX = 256
COLS = 512
MODEL = 16384
FF = 3328
FAR_FIRST = (4, 3, 5, 2, 6, 1, 7, 0)
HOPS = lambda o: min(o[0], Z - o[0]) + min(o[1], Y - o[1])
OTHERS = sorted(((d, e) for d in range(Z) for e in range(Y) if d or e), key=HOPS, reverse=True)


def slot_of(d, e):
    return (Z - d) % Z * Y + (Y - e) % Y - 1


SCALE = 1.0 / math.sqrt(HD)
LOW = -1e30


def drain(ref, sem):
    pltpu.make_async_copy(ref, ref, sem).wait()


def by_width(c, body):
    @pl.when(c < 6)
    def _():
        body(3)

    @pl.when(c >= 6)
    def _():
        body(4)


def start_of(c):
    return pl.multiple_of(c * 384 + jnp.maximum(c - 6, 0) * 128, 128)


def kernel(
    lengths_in,
    q_in, k_in, v_in, nk_in, nv_in, res_in, wo_in, gain_in, wg_in, wu_in, wd_in,
    after_out, layer_out,
    lengths, qv, kb, vb, nkb, nvb, resb, wo, gainb, wg, wu, wd,
    obuf, sbuf, ra, rs, tb, gb, gf, pr, aft,
    aftb, sq, yb, yr, own_sum, zs, zr, hr, hsent, down_sum, fs, fr, lastb,
    load_sem, a_send, a_recv, b_send, b_recv, c_send, c_recv,
    sq_send, sq_recv, y_send, y_recv, z_send, z_recv, h_send, h_recv, f_send, f_recv, out_sem,
):
    kv, tp = lax.axis_index("kv"), lax.axis_index("tp")
    z, y = kv // Y, kv % Y
    x, core = tp // 2, tp % 2

    barrier = pltpu.get_barrier_semaphore()

    @pl.loop(1, KV)
    def _(i):
        pl.semaphore_signal(barrier, inc=1, device_id=(lax.rem(kv + i, KV), tp), device_id_type=MESH)

    @pl.loop(1, TP)
    def _(i):
        pl.semaphore_signal(barrier, inc=1, device_id=(kv, lax.rem(tp + i, TP)), device_id_type=MESH)

    pairs = (
        (lengths_in, lengths), (q_in, qv), (k_in, kb), (v_in, vb), (nk_in, nkb), (nv_in, nvb), (res_in, resb), (gain_in, gainb),
        (wo_in, wo), (wg_in, wg), (wu_in, wu), (wd_in, wd),
    )
    loads = [pltpu.make_async_copy(a, b, load_sem.at[i]) for i, (a, b) in enumerate(pairs)]
    for copy in loads:
        copy.start()
    l_len, l_q, l_k, l_v, l_nk, l_nv, l_res, l_gain, l_wo, l_wg, l_wu, l_wd = loads

    def send(src, dst, send_sem, recv_sem, to):
        pltpu.make_async_remote_copy(
            src_ref=src, dst_ref=dst, send_sem=send_sem, recv_sem=recv_sem, device_id=to, device_id_type=MESH
        ).start()

    def of_plane(d, e):
        return lax.rem(z + d, Z) * Y + lax.rem(y + e, Y)

    l_len.wait()
    l_q.wait()
    l_k.wait()
    l_v.wait()
    position = lax.broadcasted_iota(jnp.int32, (STEPS * HEADS, CTX), 1) + kv * CTX
    lane = lax.broadcasted_iota(jnp.int32, (128, 128), 1)
    stats = jnp.zeros((128, 128), F32)
    for s in range(SEQS):
        rows = qv[s * STEPS : (s + 1) * STEPS].reshape(STEPS * HEADS, HD)
        scores = lax.dot_general(rows, kb[s], (((1,), (1,)), ((), ())), preferred_element_type=F32) * SCALE
        inside = position < lengths[s]
        scores = jnp.where(inside, scores, LOW)
        top = jnp.max(scores, axis=1, keepdims=True)
        weights = jnp.where(inside, jnp.exp(scores - top), 0.0)
        total = jnp.sum(weights, axis=1, keepdims=True)
        sums = jnp.dot(weights.astype(BF16), vb[s], preferred_element_type=F32)
        obuf[s * STEPS : (s + 1) * STEPS] = sums.reshape(STEPS, HEADS, HD).astype(BF16)
        stats = jnp.where(lane == s, jnp.concatenate([top, total], axis=0), stats)
    turned = stats.T
    for s in range(SEQS):
        sbuf[s] = turned[s : s + 1]

    pl.semaphore_wait(barrier, KV - 1 + TP - 1)

    for d, e in OTHERS:
        to = of_plane(d, e)
        send(sbuf.at[to // Y], rs.at[slot_of(d, e)], a_send.at[0], a_recv.at[0], (to, tp))
        send(obuf.at[to], ra.at[slot_of(d, e)], a_send.at[1], a_recv.at[1], (to, tp))

    l_nk.wait()
    l_nv.wait()
    own_q = qv[kv].astype(F32)
    fresh_k, fresh_v = nkb[z].astype(F32), nvb[z].astype(F32)
    fresh = []
    for u in range(STEPS):
        score = jnp.sum(own_q * fresh_k[u : u + 1], axis=1, keepdims=True) * SCALE
        fresh.append(jnp.where(u <= y, score, LOW))
    rs[KV - 1] = sbuf[z]
    drain(rs.at[0 : KV - 1], a_recv.at[0])
    tb[:, 0:KV] = rs[...].reshape(KV, 128).T
    tops = tb[pl.ds(pl.multiple_of(y * HEADS, HEADS), HEADS), 0:KV]
    totals = tb[pl.ds(pl.multiple_of(64 + y * HEADS, HEADS), HEADS), 0:KV]
    row_max = jnp.max(tops, axis=1, keepdims=True)
    for score in fresh:
        row_max = jnp.maximum(row_max, score)
    factor = jnp.exp(tops - row_max)
    denominator = jnp.sum(factor * totals, axis=1, keepdims=True)
    numerator = factor[:, KV - 1 : KV] * obuf[kv].astype(F32)
    for u in range(STEPS):
        weight = jnp.where(u <= y, jnp.exp(fresh[u] - row_max), 0.0)
        denominator += weight
        numerator += weight.astype(BF16).astype(F32) * fresh_v[u : u + 1]
    drain(ra, a_recv.at[1])
    for j in range(KV - 1):
        numerator += factor[:, j : j + 1] * ra[j].astype(F32)
    gb[kv] = (numerator / denominator).astype(BF16)

    for d, e in OTHERS:
        send(gb.at[kv], gb.at[kv], b_send, b_recv, (of_plane(d, e), tp))

    l_wo.wait()
    l_res.wait()
    l_gain.wait()
    drain(gb.at[0 : KV - 1], b_recv)
    gf[...] = gb[...].astype(F32).reshape(KV * HEADS, HD)
    attended = jnp.concatenate(
        [gf[pl.ds(h, KV, stride=HEADS), :].astype(BF16) for h in range(HEADS)], axis=1
    )
    pr[tp] = jnp.dot(attended, wo[...], preferred_element_type=F32).astype(BF16)

    for i in FAR_FIRST[:-1]:
        send(pr.at[tp], pr.at[tp], c_send, c_recv, (kv, lax.rem(tp + i, TP)))

    drain(pr.at[0 : TP - 1], c_recv)
    summed = resb[...].astype(F32)
    for t in range(TP):
        summed += pr[t].astype(F32)
    after = summed.astype(BF16)
    wide = after.astype(F32)
    aft[...] = wide
    aftb[...] = after
    put_after = pltpu.make_async_copy(aftb, after_out, out_sem.at[0])
    put_after.start()

    squares = jnp.broadcast_to(jnp.sum(wide * wide, axis=1, keepdims=True), (KV, 128)).T
    sq[KV - 1, :, 0:KV] = squares[0:1]
    for d, e in OTHERS:
        send(sq.at[KV - 1], sq.at[slot_of(d, e)], sq_send, sq_recv, (of_plane(d, e), tp))

    normed = jnp.concatenate(
        [wide[:, j * 128 : (j + 1) * 128] * gainb[j : j + 1].astype(F32) for j in range(COLS // 128)], axis=1
    ).astype(BF16)

    def multiply(d):
        c = lax.rem(z + d, Z)

        def body(n):
            gate = jnp.dot(normed, wg[:, pl.ds(start_of(c), n * 128)], preferred_element_type=F32)
            up = jnp.dot(normed, wu[:, pl.ds(start_of(c), n * 128)], preferred_element_type=F32)
            for i in range(n):
                for half, value in enumerate((gate, up)):
                    tile = value[:, i * 128 : (i + 1) * 128].reshape(Y, 8, 128)
                    yb[d, :, :, i * 256 + half * 128 : i * 256 + half * 128 + 128] = tile.astype(BF16)
            for e in (2, 1, 3):
                send(
                    yb.at[d, lax.rem(y + e, Y), :, 0 : n * 256],
                    yr.at[d, Y - 1 - e, :, 0 : n * 256],
                    y_send.at[d],
                    y_recv.at[d],
                    (of_plane(0, e), tp),
                )

        by_width(c, body)

    l_wg.wait()
    l_wu.wait()
    for d in FAR_FIRST:
        multiply(d)

    def finish_y(d):
        c = lax.rem(z + d, Z)

        def body(n):
            n = n * 256
            drain(yr.at[d, :, :, 0:n], y_recv.at[d])
            part = yb[d, y, :, 0:n].astype(F32)
            for i in range(Y - 1):
                part += yr[d, i, :, 0:n].astype(F32)
            if d == 0:
                own_sum[:, 0:n] = part
            else:
                zs[d, :, 0:n] = part.astype(BF16)
                send(zs.at[d, :, 0:n], zr.at[Z - 1 - d, :, 0:n], z_send.at[d], z_recv, (of_plane(d, 0), tp))

        by_width(c, body)

    for d in FAR_FIRST:
        finish_y(d)

    drain(sq.at[0 : KV - 1], sq_recv)
    tb[...] = jnp.broadcast_to(jnp.sum(sq[...].reshape(KV, 128), axis=0, keepdims=True), (128, 128)).T
    inverse = lax.rsqrt(tb[pl.ds(pl.multiple_of(y * 8, 8), 8), :] / MODEL + 1e-05)

    by_width(z, lambda n: drain(zr.at[:, :, 0 : n * 256], z_recv))
    both = own_sum[...]
    for i in range(Z - 1):
        both += zr[i].astype(F32)
    for j in range(4):
        gate = both[:, j * 256 : j * 256 + 128] * inverse
        up = both[:, j * 256 + 128 : j * 256 + 256] * inverse
        hr[z, y, :, j * 128 : (j + 1) * 128] = (gate / (1.0 + jnp.exp(-gate)) * up).astype(BF16)

    def send_hidden(n):
        own = hr.at[z, y, :, 0 : n * 128]
        for d, e in OTHERS:
            send(own, own, h_send, h_recv.at[(Z - d) % Z], (of_plane(d, e), tp))

    by_width(z, send_hidden)

    def multiply_down(d):
        c = lax.rem(z + d, Z)

        def body(n):
            drain(hr.at[c, 0 : Y - (d == 0), :, 0 : n * 128], h_recv.at[d])
            hidden = hr[c, :, :, 0 : n * 128].astype(F32).reshape(KV, n * 128).astype(BF16)
            part = jnp.dot(hidden, wd[pl.ds(start_of(c), n * 128), :], preferred_element_type=F32)
            if d == 0:
                down_sum[...] = part
            else:
                down_sum[...] += part

        by_width(c, body)

    l_wd.wait()
    for d in FAR_FIRST[::-1]:
        multiply_down(d)
    down = down_sum[...]
    fs[...] = down.reshape(4, 8, COLS).astype(BF16)

    for i in FAR_FIRST[:-1]:
        to = lax.rem(tp + i, TP)
        send(fs.at[to // 2], fr.at[TP - 1 - i], f_send, f_recv, (kv, to))

    rows = aft[pl.ds(pl.multiple_of(x * 8, 8), 8), :] + fs[x].astype(F32)
    drain(fr, f_recv)
    for i in range(TP - 1):
        rows += fr[i].astype(F32)
    lastb[...] = jnp.where(core == 0, rows[0:4], rows[4:8]).astype(BF16)
    put_layer = pltpu.make_async_copy(lastb, layer_out, out_sem.at[1])
    put_layer.start()

    drain(rs.at[0 : KV - 1], a_send.at[0])
    drain(ra, a_send.at[1])
    drain(gb.at[0 : KV - 1], b_send)
    drain(pr.at[0 : TP - 1], c_send)
    drain(sq.at[0 : KV - 1], sq_send)
    for d in range(Z):

        def left(n, d=d):
            drain(yr.at[d, :, :, 0 : n * 256], y_send.at[d])
            if d:
                drain(zs.at[d, :, 0 : n * 256], z_send.at[d])

        by_width(lax.rem(z + d, Z), left)
    by_width(z, lambda n: drain(hsent.at[:, :, 0 : n * 128], h_send))
    drain(fr, f_send)
    put_after.wait()
    put_layer.wait()


def write_out(after_in, layer_in, after_out, layer_out):
    after_out[...] = after_in[...]
    layer_out[...] = layer_in[...]


def local(queries, cache_keys, cache_values, new_keys, new_values, lengths, residual, out_weight, norm_gain,
          gate_weight, up_weight, down_weight):
    hbm = pl.BlockSpec(memory_space=pl.ANY)
    vmem = pl.BlockSpec(memory_space=pltpu.VMEM)
    dma = pltpu.SemaphoreType.DMA
    after, layer = pl.pallas_call(
        kernel,
        out_shape=(jax.ShapeDtypeStruct((KV, COLS), BF16), jax.ShapeDtypeStruct((4, COLS), BF16)),
        in_specs=[hbm] * 12,
        out_specs=(hbm, hbm),
        scratch_shapes=[
            pltpu.SMEM((SEQS,), jnp.int32),
            pltpu.VMEM((KV, HEADS, HD), BF16),
            pltpu.VMEM((SEQS, CTX, HD), BF16),
            pltpu.VMEM((SEQS, CTX, HD), BF16),
            pltpu.VMEM((SEQS, STEPS, HD), BF16),
            pltpu.VMEM((SEQS, STEPS, HD), BF16),
            pltpu.VMEM((KV, COLS), BF16),
            pltpu.VMEM((HEADS * HD, COLS), BF16),
            pltpu.VMEM((4, 128), BF16),
            pltpu.VMEM((COLS, FF), BF16),
            pltpu.VMEM((COLS, FF), BF16),
            pltpu.VMEM((FF, COLS), BF16),
            pltpu.VMEM((KV, HEADS, HD), BF16),
            pltpu.VMEM((SEQS, 1, 128), F32),
            pltpu.VMEM((KV - 1, HEADS, HD), BF16),
            pltpu.VMEM((KV, 1, 128), F32),
            pltpu.VMEM((128, 128), F32),
            pltpu.VMEM((KV, HEADS, HD), BF16),
            pltpu.VMEM((KV * HEADS, HD), F32),
            pltpu.VMEM((TP, KV, COLS), BF16),
            pltpu.VMEM((KV, COLS), F32),
            pltpu.VMEM((KV, COLS), BF16),
            pltpu.VMEM((KV, 1, 128), F32),
            pltpu.VMEM((Z, Y, 8, 1024), BF16),
            pltpu.VMEM((Z, Y - 1, 8, 1024), BF16),
            pltpu.VMEM((8, 1024), F32),
            pltpu.VMEM((Z, 8, 1024), BF16),
            pltpu.VMEM((Z - 1, 8, 1024), BF16),
            pltpu.VMEM((Z, Y, 8, 512), BF16),
            pltpu.VMEM((KV - 1, 8, 512), BF16),
            pltpu.VMEM((KV, COLS), F32),
            pltpu.VMEM((4, 8, COLS), BF16),
            pltpu.VMEM((TP - 1, 8, COLS), BF16),
            pltpu.VMEM((4, COLS), BF16),
            dma((12,)), dma((2,)), dma((2,)), dma, dma, dma, dma,
            dma, dma, dma((Z,)), dma((Z,)), dma((Z,)), dma, dma, dma((Z,)), dma, dma, dma((2,)),
        ],
        compiler_params=pltpu.CompilerParams(
            collective_id=0, has_side_effects=True, vmem_limit_bytes=60 * 1024 * 1024
        ),
    )(
        lengths,
        queries.reshape(KV, HEADS, HD),
        cache_keys.reshape(SEQS, CTX, HD),
        cache_values.reshape(SEQS, CTX, HD),
        new_keys.reshape(SEQS, STEPS, HD),
        new_values.reshape(SEQS, STEPS, HD),
        residual,
        out_weight,
        norm_gain.reshape(4, 128),
        gate_weight,
        up_weight,
        down_weight,
    )
    return pl.pallas_call(
        write_out,
        out_shape=(jax.ShapeDtypeStruct((KV, COLS), BF16), jax.ShapeDtypeStruct((4, COLS), BF16)),
        in_specs=[vmem, vmem],
        out_specs=(vmem, vmem),
    )(after, layer)


def solution(mesh):
    return jax.shard_map(
        local,
        mesh=mesh,
        in_specs=(
            P(None, None, "tp", None),
            P(None, "kv", "tp", None),
            P(None, "kv", "tp", None),
            P(None, None, "tp", None),
            P(None, None, "tp", None),
            P(),
            P(None, "kv"),
            P("tp", "kv"),
            P("kv"),
            P("kv", "tp"),
            P("kv", "tp"),
            P("tp", "kv"),
        ),
        out_specs=(P(None, "kv"), P("tp", "kv")),
        check_vma=False,
    )
```

time: 63.8 us -> 55.1 us (0.86)
  Pallas kernels: 59.1 us -> 54.3 us
  local copies, waits for them, and re-layouts: 2.65 us -> 0 us
  other arithmetic: 1.26 us -> 0 us
    pallas_call x1, Pallas kernels: 59.1 us -> 52.9 us  [local(): pl.pallas_call(kernel, out_shape=(jax.ShapeDtypeStruct((KV, COLS), BF16),...]
    unnamed x2 -> x0, local copies, waits for them, and re-layouts: 2.65 us -> none
    pallas_call x0 -> x1, Pallas kernels: none -> 1.38 us  [local(): pl.pallas_call(write_out, out_shape=(jax.ShapeDtypeStruct((KV, COLS), BF1...]
    reshape x1 -> x0, other arithmetic: 1.26 us -> none  [local(): norm_gain.astype(F32).reshape(1, COLS)]
where the time goes in v2:
time: 55.1 us; the launch traced here: 54.9 us
  Pallas kernels  54.3 us (99%)
  between operations  0.64 us (1%)
    pallas_call x1, Pallas kernels, local(): pl.pallas_call(kernel, out_shape=(jax.ShapeDtypeStruct((KV, COLS), BF16),...  52.9 us
    pallas_call x1, Pallas kernels, local(): pl.pallas_call(write_out, out_shape=(jax.ShapeDtypeStruct((KV, COLS), BF1...  1.38 us

profile of v2, /device:TPU:1, one launch (start us, length us, event | category | flops | bytes accessed | tf_op | source)
XLA Modules:
  0.0 54.9 jit_solution(4003553097853248154)
XLA Ops:
  0.6 52.9 %shard_map.131 = (bf16[32,512]{1,0:T(8,128)(2,1)}, bf16[4,512]{1,0:T(4,128)(2,1)}) custom-call(s32[8]{0:T(128)} %lengths_in.1, bf16[32,16,128]{2,1,0:T(8,128)(2,1)} %bitcast.8, bf16[8,256,128]{2,1,0:T(8,128)(2,1)} %bitcast.6, bf16[8,256,128]{2,1,0:T(8,128)(2,1)} %bitcast.7, bf16[8,4,128]{2,1,0:T(4,128)(2,1)} %bitcast.9, bf16[8,4,128]{2,1,0:T(4,128)(2,1)} %bitcast.10, ...), custom_call_target="tpu_custom_call" | custom-call | tf_op jit(solution)/shard_map/pallas_call | solution.py:311
  53.6 1.4 %shard_map.132 = (bf16[32,512]{1,0:T(8,128)(2,1)}, bf16[4,512]{1,0:T(4,128)(2,1)}) custom-call(bf16[32,512]{1,0:T(8,128)(2,1)} %get-tuple-element.4.after_in, bf16[4,512]{1,0:T(4,128)(2,1)} %get-tuple-element.5.layer_in), custom_call_target="tpu_custom_call" | custom-call | tf_op jit(solution)/shard_map/pallas_call | solution.py:371

commit v3 on v2

--- a/solution.py
+++ b/solution.py
@@ -53,31 +53,19 @@
     after_out, layer_out,
     lengths, qv, kb, vb, nkb, nvb, resb, wo, gainb, wg, wu, wd,
     obuf, sbuf, ra, rs, tb, gb, gf, pr, aft,
-    aftb, sq, yb, yr, own_sum, zs, zr, hr, hsent, down_sum, fs, fr, lastb,
+    sq, yb, yr, own_sum, zs, zr, hr, hsent, down_sum, fs, fr,
     load_sem, a_send, a_recv, b_send, b_recv, c_send, c_recv,
-    sq_send, sq_recv, y_send, y_recv, z_send, z_recv, h_send, h_recv, f_send, f_recv, out_sem,
+    sq_send, sq_recv, y_send, y_recv, z_send, z_recv, h_send, h_recv, f_send, f_recv,
 ):
     kv, tp = lax.axis_index("kv"), lax.axis_index("tp")
     z, y = kv // Y, kv % Y
     x, core = tp // 2, tp % 2
-
-    barrier = pltpu.get_barrier_semaphore()
-
-    @pl.loop(1, KV)
-    def _(i):
-        pl.semaphore_signal(barrier, inc=1, device_id=(lax.rem(kv + i, KV), tp), device_id_type=MESH)
-
-    @pl.loop(1, TP)
-    def _(i):
-        pl.semaphore_signal(barrier, inc=1, device_id=(kv, lax.rem(tp + i, TP)), device_id_type=MESH)
 
     pairs = (
         (lengths_in, lengths), (q_in, qv), (k_in, kb), (v_in, vb), (nk_in, nkb), (nv_in, nvb), (res_in, resb), (gain_in, gainb),
         (wo_in, wo), (wg_in, wg), (wu_in, wu), (wd_in, wd),
     )
     loads = [pltpu.make_async_copy(a, b, load_sem.at[i]) for i, (a, b) in enumerate(pairs)]
-    for copy in loads:
-        copy.start()
     l_len, l_q, l_k, l_v, l_nk, l_nv, l_res, l_gain, l_wo, l_wg, l_wu, l_wd = loads
 
     def send(src, dst, send_sem, recv_sem, to):
@@ -87,6 +75,23 @@
 
     def of_plane(d, e):
         return lax.rem(z + d, Z) * Y + lax.rem(y + e, Y)
+
+    for copy in loads[:4]:
+        copy.start()
+    barrier = pltpu.get_barrier_semaphore()
+
+    @pl.loop(0, KV - 1)
+    def _(i):
+        j = i // Y
+        d = 4 + j // 2 - j % 2 * (j // 2 * 2 + 1)
+        pl.semaphore_signal(barrier, inc=1, device_id=(of_plane(d, (i + 1) % Y), tp), device_id_type=MESH)
+
+    @pl.loop(1, TP)
+    def _(i):
+        pl.semaphore_signal(barrier, inc=1, device_id=(kv, lax.rem(tp + i, TP)), device_id_type=MESH)
+
+    for copy in loads[4:]:
+        copy.start()
 
     l_len.wait()
     l_q.wait()
@@ -168,25 +173,25 @@
     after = summed.astype(BF16)
     wide = after.astype(F32)
     aft[...] = wide
-    aftb[...] = after
-    put_after = pltpu.make_async_copy(aftb, after_out, out_sem.at[0])
-    put_after.start()
-
-    squares = jnp.broadcast_to(jnp.sum(wide * wide, axis=1, keepdims=True), (KV, 128)).T
-    sq[KV - 1, :, 0:KV] = squares[0:1]
-    for d, e in OTHERS:
-        send(sq.at[KV - 1], sq.at[slot_of(d, e)], sq_send, sq_recv, (of_plane(d, e), tp))
+    after_out[...] = after
 
     normed = jnp.concatenate(
         [wide[:, j * 128 : (j + 1) * 128] * gainb[j : j + 1].astype(F32) for j in range(COLS // 128)], axis=1
     ).astype(BF16)
 
+    def send_squares():
+        squares = jnp.broadcast_to(jnp.sum(wide * wide, axis=1, keepdims=True), (KV, 128)).T
+        sq[KV - 1, :, 0:KV] = squares[0:1]
+        for d, e in OTHERS:
+            send(sq.at[KV - 1], sq.at[slot_of(d, e)], sq_send, sq_recv, (of_plane(d, e), tp))
+
     def multiply(d):
         c = lax.rem(z + d, Z)
 
         def body(n):
-            gate = jnp.dot(normed, wg[:, pl.ds(start_of(c), n * 128)], preferred_element_type=F32)
-            up = jnp.dot(normed, wu[:, pl.ds(start_of(c), n * 128)], preferred_element_type=F32)
+            block = pl.ds(start_of(c), n * 128)
+            gate = jnp.dot(normed, wg[:, block], preferred_element_type=F32)
+            up = jnp.dot(normed, wu[:, block], preferred_element_type=F32)
             for i in range(n):
                 for half, value in enumerate((gate, up)):
                     tile = value[:, i * 128 : (i + 1) * 128].reshape(Y, 8, 128)
@@ -206,6 +211,8 @@
     l_wu.wait()
     for d in FAR_FIRST:
         multiply(d)
+        if d == FAR_FIRST[1]:
+            send_squares()
 
     def finish_y(d):
         c = lax.rem(z + d, Z)
@@ -275,9 +282,7 @@
     drain(fr, f_recv)
     for i in range(TP - 1):
         rows += fr[i].astype(F32)
-    lastb[...] = jnp.where(core == 0, rows[0:4], rows[4:8]).astype(BF16)
-    put_layer = pltpu.make_async_copy(lastb, layer_out, out_sem.at[1])
-    put_layer.start()
+    layer_out[...] = jnp.where(core == 0, rows[0:4], rows[4:8]).astype(BF16)
 
     drain(rs.at[0 : KV - 1], a_send.at[0])
     drain(ra, a_send.at[1])
@@ -294,13 +299,17 @@
         by_width(lax.rem(z + d, Z), left)
     by_width(z, lambda n: drain(hsent.at[:, :, 0 : n * 128], h_send))
     drain(fr, f_send)
-    put_after.wait()
-    put_layer.wait()
-
-
-def write_out(after_in, layer_in, after_out, layer_out):
-    after_out[...] = after_in[...]
-    layer_out[...] = layer_in[...]
+
+
+def write_out(after_in, layer_in, after_out, layer_out, sem):
+    copies = [
+        pltpu.make_async_copy(after_in, after_out, sem.at[0]),
+        pltpu.make_async_copy(layer_in, layer_out, sem.at[1]),
+    ]
+    for copy in copies:
+        copy.start()
+    for copy in copies:
+        copy.wait()
 
 
 def local(queries, cache_keys, cache_values, new_keys, new_values, lengths, residual, out_weight, norm_gain,
@@ -310,9 +319,9 @@
     dma = pltpu.SemaphoreType.DMA
     after, layer = pl.pallas_call(
         kernel,
-        out_shape=(jax.ShapeDtypeStruct((KV, COLS), BF16), jax.ShapeDtypeStruct((4, COLS), BF16)),
+        out_shape=(pltpu.VMEM((KV, COLS), BF16), pltpu.VMEM((4, COLS), BF16)),
         in_specs=[hbm] * 12,
-        out_specs=(hbm, hbm),
+        out_specs=(vmem, vmem),
         scratch_shapes=[
             pltpu.SMEM((SEQS,), jnp.int32),
             pltpu.VMEM((KV, HEADS, HD), BF16),
@@ -335,7 +344,6 @@
             pltpu.VMEM((KV * HEADS, HD), F32),
             pltpu.VMEM((TP, KV, COLS), BF16),
             pltpu.VMEM((KV, COLS), F32),
-            pltpu.VMEM((KV, COLS), BF16),
             pltpu.VMEM((KV, 1, 128), F32),
             pltpu.VMEM((Z, Y, 8, 1024), BF16),
             pltpu.VMEM((Z, Y - 1, 8, 1024), BF16),
@@ -347,32 +355,38 @@
             pltpu.VMEM((KV, COLS), F32),
             pltpu.VMEM((4, 8, COLS), BF16),
             pltpu.VMEM((TP - 1, 8, COLS), BF16),
-            pltpu.VMEM((4, COLS), BF16),
             dma((12,)), dma((2,)), dma((2,)), dma, dma, dma, dma,
-            dma, dma, dma((Z,)), dma((Z,)), dma((Z,)), dma, dma, dma((Z,)), dma, dma, dma((2,)),
+            dma, dma, dma((Z,)), dma((Z,)), dma((Z,)), dma, dma, dma((Z,)), dma, dma,
         ],
         compiler_params=pltpu.CompilerParams(
             collective_id=0, has_side_effects=True, vmem_limit_bytes=60 * 1024 * 1024
         ),
     )(
-        lengths,
-        queries.reshape(KV, HEADS, HD),
-        cache_keys.reshape(SEQS, CTX, HD),
-        cache_values.reshape(SEQS, CTX, HD),
-        new_keys.reshape(SEQS, STEPS, HD),
-        new_values.reshape(SEQS, STEPS, HD),
-        residual,
-        out_weight,
-        norm_gain.reshape(4, 128),
-        gate_weight,
-        up_weight,
-        down_weight,
+        *(
+            pltpu.with_memory_space_constraint(array, pltpu.HBM)
+            for array in (
+                lengths,
+                queries.reshape(KV, HEADS, HD),
+                cache_keys.reshape(SEQS, CTX, HD),
+                cache_values.reshape(SEQS, CTX, HD),
+                new_keys.reshape(SEQS, STEPS, HD),
+                new_values.reshape(SEQS, STEPS, HD),
+                residual,
+                out_weight,
+                norm_gain.reshape(4, 128),
+                gate_weight,
+                up_weight,
+                down_weight,
+            )
+        )
     )
     return pl.pallas_call(
         write_out,
         out_shape=(jax.ShapeDtypeStruct((KV, COLS), BF16), jax.ShapeDtypeStruct((4, COLS), BF16)),
         in_specs=[vmem, vmem],
-        out_specs=(vmem, vmem),
+        out_specs=(hbm, hbm),
+        scratch_shapes=[dma((2,))],
+        compiler_params=pltpu.CompilerParams(vmem_limit_bytes=1024 * 1024),
     )(after, layer)
 
 

time: 55.1 us -> 53.4 us (0.969)
  Pallas kernels: 54.3 us -> 52.7 us
    pallas_call x1, Pallas kernels: 52.9 us -> 52.1 us  [local(): pl.pallas_call(kernel, out_shape=(pltpu.VMEM((KV, COLS), BF16), pltpu.VME...]
    pallas_call x1, Pallas kernels: 1.38 us -> 0.64 us  [local(): pl.pallas_call(write_out, out_shape=(jax.ShapeDtypeStruct((KV, COLS), BF1...]
where the time goes in v3:
time: 53.4 us; the launch traced here: 53.3 us
  Pallas kernels  52.7 us (99%)
  between operations  0.64 us (1%)
    pallas_call x1, Pallas kernels, local(): pl.pallas_call(kernel, out_shape=(pltpu.VMEM((KV, COLS), BF16), pltpu.VME...  52.1 us

profile of v3, /device:TPU:1, one launch (start us, length us, event | category | flops | bytes accessed | tf_op | source)
XLA Modules:
  0.0 53.3 jit_solution(16444702495406831957)
XLA Ops:
  0.6 52.1 %shard_map.131 = (bf16[32,512]{1,0:T(8,128)(2,1)S(1)}, bf16[4,512]{1,0:T(4,128)(2,1)S(1)}) custom-call(s32[8]{0:T(128)} %lengths_in.1, bf16[32,16,128]{2,1,0:T(8,128)(2,1)} %bitcast.8, bf16[8,256,128]{2,1,0:T(8,128)(2,1)} %bitcast.6, bf16[8,256,128]{2,1,0:T(8,128)(2,1)} %bitcast.7, bf16[8,4,128]{2,1,0:T(4,128)(2,1)} %bitcast.9, bf16[8,4,128]{2,1,0:T(4,128)(2,1)} %bitcast.10, ...), custom_call_target="tpu_custom_call" | custom-call | tf_op jit(solution)/shard_map/pallas_call | solution.py:320
  52.7 0.6 %shard_map.132 = (bf16[32,512]{1,0:T(8,128)(2,1)}, bf16[4,512]{1,0:T(4,128)(2,1)}) custom-call(bf16[32,512]{1,0:T(8,128)(2,1)S(1)} %get-tuple-element.4.after_in, bf16[4,512]{1,0:T(4,128)(2,1)S(1)} %get-tuple-element.5.layer_in), custom_call_target="tpu_custom_call" | custom-call | tf_op jit(solution)/shard_map/pallas_call | solution.py:383

commit v4 on v3

--- a/solution.py
+++ b/solution.py
@@ -16,7 +16,9 @@
 COLS = 512
 MODEL = 16384
 FF = 3328
+WIDTH = (3, 3, 3, 3, 3, 3, 4, 4)
 FAR_FIRST = (4, 3, 5, 2, 6, 1, 7, 0)
+NEAR = (1, 7)
 HOPS = lambda o: min(o[0], Z - o[0]) + min(o[1], Y - o[1])
 OTHERS = sorted(((d, e) for d in range(Z) for e in range(Y) if d or e), key=HOPS, reverse=True)
 
@@ -53,9 +55,9 @@
     after_out, layer_out,
     lengths, qv, kb, vb, nkb, nvb, resb, wo, gainb, wg, wu, wd,
     obuf, sbuf, ra, rs, tb, gb, gf, pr, aft,
-    sq, yb, yr, own_sum, zs, zr, hr, hsent, down_sum, fs, fr,
+    sq, yb, yr, own_part, own_sum, nr, zs, zr, hr, hsent, fs, fr,
     load_sem, a_send, a_recv, b_send, b_recv, c_send, c_recv,
-    sq_send, sq_recv, y_send, y_recv, z_send, z_recv, h_send, h_recv, f_send, f_recv,
+    sq_send, sq_recv, y_send, y_recv, n_recv, z_send, z_recv, h_send, h_recv, f_send, f_recv,
 ):
     kv, tp = lax.axis_index("kv"), lax.axis_index("tp")
     z, y = kv // Y, kv % Y
@@ -162,7 +164,6 @@
         [gf[pl.ds(h, KV, stride=HEADS), :].astype(BF16) for h in range(HEADS)], axis=1
     )
     pr[tp] = jnp.dot(attended, wo[...], preferred_element_type=F32).astype(BF16)
-
     for i in FAR_FIRST[:-1]:
         send(pr.at[tp], pr.at[tp], c_send, c_recv, (kv, lax.rem(tp + i, TP)))
 
@@ -185,6 +186,24 @@
         for d, e in OTHERS:
             send(sq.at[KV - 1], sq.at[slot_of(d, e)], sq_send, sq_recv, (of_plane(d, e), tp))
 
+    def send_y(d, n):
+        for e in (2, 1, 3):
+            send(
+                yb.at[d, lax.rem(y + e, Y), :, 0 : n * 256],
+                yr.at[d, Y - 1 - e, :, 0 : n * 256],
+                y_send.at[d],
+                y_recv.at[d],
+                (of_plane(0, e), tp),
+            )
+
+    def add_near(n):
+        for i in range(2):
+            drain(nr.at[i, :, :, 0 : n * 256], n_recv.at[i])
+        part = own_part[:, :, 0 : n * 256] + nr[0, :, :, 0 : n * 256].astype(F32) + nr[1, :, :, 0 : n * 256].astype(F32)
+        own_part[:, :, 0 : n * 256] = part
+        yb[0, :, :, 0 : n * 256] = part.astype(BF16)
+        send_y(0, n)
+
     def multiply(d):
         c = lax.rem(z + d, Z)
 
@@ -195,15 +214,21 @@
             for i in range(n):
                 for half, value in enumerate((gate, up)):
                     tile = value[:, i * 128 : (i + 1) * 128].reshape(Y, 8, 128)
-                    yb[d, :, :, i * 256 + half * 128 : i * 256 + half * 128 + 128] = tile.astype(BF16)
-            for e in (2, 1, 3):
+                    at = i * 256 + half * 128
+                    if d == 0:
+                        own_part[:, :, at : at + 128] = tile
+                    else:
+                        yb[d, :, :, at : at + 128] = tile.astype(BF16)
+            if d in NEAR:
                 send(
-                    yb.at[d, lax.rem(y + e, Y), :, 0 : n * 256],
-                    yr.at[d, Y - 1 - e, :, 0 : n * 256],
+                    yb.at[d, :, :, 0 : n * 256],
+                    nr.at[NEAR.index(d), :, :, 0 : n * 256],
                     y_send.at[d],
-                    y_recv.at[d],
-                    (of_plane(0, e), tp),
+                    n_recv.at[NEAR.index(d)],
+                    (of_plane(d, 0), tp),
                 )
+            elif d:
+                send_y(d, n)
 
         by_width(c, body)
 
@@ -220,18 +245,21 @@
         def body(n):
             n = n * 256
             drain(yr.at[d, :, :, 0:n], y_recv.at[d])
-            part = yb[d, y, :, 0:n].astype(F32)
+            part = yb[d, y, :, 0:n].astype(F32) if d else own_part[y, :, 0:n]
             for i in range(Y - 1):
                 part += yr[d, i, :, 0:n].astype(F32)
             if d == 0:
                 own_sum[:, 0:n] = part
             else:
                 zs[d, :, 0:n] = part.astype(BF16)
-                send(zs.at[d, :, 0:n], zr.at[Z - 1 - d, :, 0:n], z_send.at[d], z_recv, (of_plane(d, 0), tp))
+                send(zs.at[d, :, 0:n], zr.at[6 - d, :, 0:n], z_send.at[d], z_recv, (of_plane(d, 0), tp))
 
         by_width(c, body)
 
-    for d in FAR_FIRST:
+    for d in (4, 3, 5):
+        finish_y(d)
+    by_width(z, add_near)
+    for d in (2, 6, 0):
         finish_y(d)
 
     drain(sq.at[0 : KV - 1], sq_recv)
@@ -240,7 +268,7 @@
 
     by_width(z, lambda n: drain(zr.at[:, :, 0 : n * 256], z_recv))
     both = own_sum[...]
-    for i in range(Z - 1):
+    for i in range(Z - 3):
         both += zr[i].astype(F32)
     for j in range(4):
         gate = both[:, j * 256 : j * 256 + 128] * inverse
@@ -254,24 +282,14 @@
 
     by_width(z, send_hidden)
 
-    def multiply_down(d):
+    l_wd.wait()
+    for d in (0, 4, 3, 5, 2, 6, 1, 7):
         c = lax.rem(z + d, Z)
-
-        def body(n):
-            drain(hr.at[c, 0 : Y - (d == 0), :, 0 : n * 128], h_recv.at[d])
-            hidden = hr[c, :, :, 0 : n * 128].astype(F32).reshape(KV, n * 128).astype(BF16)
-            part = jnp.dot(hidden, wd[pl.ds(start_of(c), n * 128), :], preferred_element_type=F32)
-            if d == 0:
-                down_sum[...] = part
-            else:
-                down_sum[...] += part
-
-        by_width(c, body)
-
-    l_wd.wait()
-    for d in FAR_FIRST[::-1]:
-        multiply_down(d)
-    down = down_sum[...]
+        by_width(c, lambda n, c=c, d=d: drain(hr.at[c, 0 : Y - (d == 0), :, 0 : n * 128], h_recv.at[d]))
+    hidden = jnp.concatenate(
+        [hr[c, :, :, 0 : WIDTH[c] * 128].astype(F32).reshape(KV, WIDTH[c] * 128).astype(BF16) for c in range(Z)], axis=1
+    )
+    down = jnp.dot(hidden, wd[...], preferred_element_type=F32)
     fs[...] = down.reshape(4, 8, COLS).astype(BF16)
 
     for i in FAR_FIRST[:-1]:
@@ -292,8 +310,8 @@
     for d in range(Z):
 
         def left(n, d=d):
-            drain(yr.at[d, :, :, 0 : n * 256], y_send.at[d])
-            if d:
+            drain(yb.at[d, 0 : Y - (d not in NEAR), :, 0 : n * 256], y_send.at[d])
+            if d and d not in NEAR:
                 drain(zs.at[d, :, 0 : n * 256], z_send.at[d])
 
         by_width(lax.rem(z + d, Z), left)
@@ -347,16 +365,17 @@
             pltpu.VMEM((KV, 1, 128), F32),
             pltpu.VMEM((Z, Y, 8, 1024), BF16),
             pltpu.VMEM((Z, Y - 1, 8, 1024), BF16),
+            pltpu.VMEM((Y, 8, 1024), F32),
             pltpu.VMEM((8, 1024), F32),
+            pltpu.VMEM((2, Y, 8, 1024), BF16),
             pltpu.VMEM((Z, 8, 1024), BF16),
-            pltpu.VMEM((Z - 1, 8, 1024), BF16),
+            pltpu.VMEM((Z - 3, 8, 1024), BF16),
             pltpu.VMEM((Z, Y, 8, 512), BF16),
             pltpu.VMEM((KV - 1, 8, 512), BF16),
-            pltpu.VMEM((KV, COLS), F32),
             pltpu.VMEM((4, 8, COLS), BF16),
             pltpu.VMEM((TP - 1, 8, COLS), BF16),
             dma((12,)), dma((2,)), dma((2,)), dma, dma, dma, dma,
-            dma, dma, dma((Z,)), dma((Z,)), dma((Z,)), dma, dma, dma((Z,)), dma, dma,
+            dma, dma, dma((Z,)), dma((Z,)), dma((2,)), dma((Z,)), dma, dma, dma((Z,)), dma, dma,
         ],
         compiler_params=pltpu.CompilerParams(
             collective_id=0, has_side_effects=True, vmem_limit_bytes=60 * 1024 * 1024

time: 53.4 us -> 52.5 us (0.983)
  Pallas kernels: 52.7 us -> 51.7 us
    pallas_call x1, Pallas kernels: 52.1 us -> 51.1 us  [local(): pl.pallas_call(kernel, out_shape=(pltpu.VMEM((KV, COLS), BF16), pltpu.VME...]
where the time goes in v4:
time: 52.5 us; the launch traced here: 52.4 us
  Pallas kernels  51.7 us (98%)
  between operations  0.64 us (1%)
    pallas_call x1, Pallas kernels, local(): pl.pallas_call(kernel, out_shape=(pltpu.VMEM((KV, COLS), BF16), pltpu.VME...  51.1 us

profile of v4, /device:TPU:1, one launch (start us, length us, event | category | flops | bytes accessed | tf_op | source)
XLA Modules:
  0.0 52.4 jit_solution(18415189115231296355)
XLA Ops:
  0.6 51.1 %shard_map.131 = (bf16[32,512]{1,0:T(8,128)(2,1)S(1)}, bf16[4,512]{1,0:T(4,128)(2,1)S(1)}) custom-call(s32[8]{0:T(128)} %lengths_in.1, bf16[32,16,128]{2,1,0:T(8,128)(2,1)} %bitcast.8, bf16[8,256,128]{2,1,0:T(8,128)(2,1)} %bitcast.6, bf16[8,256,128]{2,1,0:T(8,128)(2,1)} %bitcast.7, bf16[8,4,128]{2,1,0:T(4,128)(2,1)} %bitcast.9, bf16[8,4,128]{2,1,0:T(4,128)(2,1)} %bitcast.10, ...), custom_call_target="tpu_custom_call" | custom-call | tf_op jit(solution)/shard_map/pallas_call | solution.py:338
  51.7 0.6 %shard_map.132 = (bf16[32,512]{1,0:T(8,128)(2,1)}, bf16[4,512]{1,0:T(4,128)(2,1)}) custom-call(bf16[32,512]{1,0:T(8,128)(2,1)S(1)} %get-tuple-element.4.after_in, bf16[4,512]{1,0:T(4,128)(2,1)S(1)} %get-tuple-element.5.layer_in), custom_call_target="tpu_custom_call" | custom-call | tf_op jit(solution)/shard_map/pallas_call | solution.py:402

commit v5 on v4

--- a/solution.py
+++ b/solution.py
@@ -19,6 +19,7 @@
 WIDTH = (3, 3, 3, 3, 3, 3, 4, 4)
 FAR_FIRST = (4, 3, 5, 2, 6, 1, 7, 0)
 NEAR = (1, 7)
+Y_STAGE = (4, 3, 5, 2, 6, 0)
 HOPS = lambda o: min(o[0], Z - o[0]) + min(o[1], Y - o[1])
 OTHERS = sorted(((d, e) for d in range(Z) for e in range(Y) if d or e), key=HOPS, reverse=True)
 
@@ -45,19 +46,14 @@
         body(4)
 
 
-def start_of(c):
-    return pl.multiple_of(c * 384 + jnp.maximum(c - 6, 0) * 128, 128)
-
-
 def kernel(
     lengths_in,
     q_in, k_in, v_in, nk_in, nv_in, res_in, wo_in, gain_in, wg_in, wu_in, wd_in,
     after_out, layer_out,
-    lengths, qv, kb, vb, nkb, nvb, resb, wo, gainb, wg, wu, wd,
+    lengths, qv, kb, vb, nkb, nvb, resb, wo, gainb, wgu, wd,
     obuf, sbuf, ra, rs, tb, gb, gf, pr, aft,
-    sq, yb, yr, own_part, own_sum, nr, zs, zr, hr, hsent, fs, fr,
-    load_sem, a_send, a_recv, b_send, b_recv, c_send, c_recv,
-    sq_send, sq_recv, y_send, y_recv, n_recv, z_send, z_recv, h_send, h_recv, f_send, f_recv,
+    sq, yb, yr, own_part, own_sum, nr, zs, zr, hr, sized, fs, fr,
+    load_sem, gu_sem, sent, a_recv, b_recv, c_recv, sq_recv, y_recv, n_recv, z_recv, h_recv, f_recv,
 ):
     kv, tp = lax.axis_index("kv"), lax.axis_index("tp")
     z, y = kv // Y, kv % Y
@@ -65,10 +61,9 @@
 
     pairs = (
         (lengths_in, lengths), (q_in, qv), (k_in, kb), (v_in, vb), (nk_in, nkb), (nv_in, nvb), (res_in, resb), (gain_in, gainb),
-        (wo_in, wo), (wg_in, wg), (wu_in, wu), (wd_in, wd),
+        (wo_in, wo), (wd_in, wd),
     )
-    loads = [pltpu.make_async_copy(a, b, load_sem.at[i]) for i, (a, b) in enumerate(pairs)]
-    l_len, l_q, l_k, l_v, l_nk, l_nv, l_res, l_gain, l_wo, l_wg, l_wu, l_wd = loads
+    loads = [pltpu.make_async_copy(a, b, load_sem.at[i]) for i, (a, b) in zip((0, 1, 1, 1, 2, 2, 3, 4, 5, 6), pairs)]
 
     def send(src, dst, send_sem, recv_sem, to):
         pltpu.make_async_remote_copy(
@@ -95,10 +90,8 @@
     for copy in loads[4:]:
         copy.start()
 
-    l_len.wait()
-    l_q.wait()
-    l_k.wait()
-    l_v.wait()
+    loads[0].wait()
+    drain(wgu.at[:, 0:1152], load_sem.at[1])
     position = lax.broadcasted_iota(jnp.int32, (STEPS * HEADS, CTX), 1) + kv * CTX
     lane = lax.broadcasted_iota(jnp.int32, (128, 128), 1)
     stats = jnp.zeros((128, 128), F32)
@@ -121,11 +114,19 @@
 
     for d, e in OTHERS:
         to = of_plane(d, e)
-        send(sbuf.at[to // Y], rs.at[slot_of(d, e)], a_send.at[0], a_recv.at[0], (to, tp))
-        send(obuf.at[to], ra.at[slot_of(d, e)], a_send.at[1], a_recv.at[1], (to, tp))
-
-    l_nk.wait()
-    l_nv.wait()
+        send(sbuf.at[to // Y], rs.at[slot_of(d, e)], sent, a_recv.at[0], (to, tp))
+        send(obuf.at[to], ra.at[slot_of(d, e)], sent, a_recv.at[1], (to, tp))
+
+    @pl.loop(0, FF // 128)
+    def _(j):
+        block = pl.ds(pl.multiple_of(j * 128, 128), 128)
+        for half, weight in enumerate((wg_in, wu_in)):
+            there = pl.ds(pl.multiple_of(j * 256 + half * 128, 128), 128)
+            pltpu.make_async_copy(weight.at[:, block], wgu.at[:, there], gu_sem).start()
+
+    drain(qv.at[0:4], load_sem.at[2])
+    for copy in loads[6:]:
+        copy.wait()
     own_q = qv[kv].astype(F32)
     fresh_k, fresh_v = nkb[z].astype(F32), nvb[z].astype(F32)
     fresh = []
@@ -134,6 +135,7 @@
         fresh.append(jnp.where(u <= y, score, LOW))
     rs[KV - 1] = sbuf[z]
     drain(rs.at[0 : KV - 1], a_recv.at[0])
+    drain(ra, a_recv.at[1])
     tb[:, 0:KV] = rs[...].reshape(KV, 128).T
     tops = tb[pl.ds(pl.multiple_of(y * HEADS, HEADS), HEADS), 0:KV]
     totals = tb[pl.ds(pl.multiple_of(64 + y * HEADS, HEADS), HEADS), 0:KV]
@@ -147,17 +149,13 @@
         weight = jnp.where(u <= y, jnp.exp(fresh[u] - row_max), 0.0)
         denominator += weight
         numerator += weight.astype(BF16).astype(F32) * fresh_v[u : u + 1]
-    drain(ra, a_recv.at[1])
     for j in range(KV - 1):
         numerator += factor[:, j : j + 1] * ra[j].astype(F32)
     gb[kv] = (numerator / denominator).astype(BF16)
 
     for d, e in OTHERS:
-        send(gb.at[kv], gb.at[kv], b_send, b_recv, (of_plane(d, e), tp))
-
-    l_wo.wait()
-    l_res.wait()
-    l_gain.wait()
+        send(gb.at[kv], gb.at[kv], sent, b_recv, (of_plane(d, e), tp))
+
     drain(gb.at[0 : KV - 1], b_recv)
     gf[...] = gb[...].astype(F32).reshape(KV * HEADS, HD)
     attended = jnp.concatenate(
@@ -165,7 +163,7 @@
     )
     pr[tp] = jnp.dot(attended, wo[...], preferred_element_type=F32).astype(BF16)
     for i in FAR_FIRST[:-1]:
-        send(pr.at[tp], pr.at[tp], c_send, c_recv, (kv, lax.rem(tp + i, TP)))
+        send(pr.at[tp], pr.at[tp], sent, c_recv, (kv, lax.rem(tp + i, TP)))
 
     drain(pr.at[0 : TP - 1], c_recv)
     summed = resb[...].astype(F32)
@@ -184,21 +182,20 @@
         squares = jnp.broadcast_to(jnp.sum(wide * wide, axis=1, keepdims=True), (KV, 128)).T
         sq[KV - 1, :, 0:KV] = squares[0:1]
         for d, e in OTHERS:
-            send(sq.at[KV - 1], sq.at[slot_of(d, e)], sq_send, sq_recv, (of_plane(d, e), tp))
+            send(sq.at[KV - 1], sq.at[slot_of(d, e)], sent, sq_recv, (of_plane(d, e), tp))
 
     def send_y(d, n):
         for e in (2, 1, 3):
             send(
                 yb.at[d, lax.rem(y + e, Y), :, 0 : n * 256],
                 yr.at[d, Y - 1 - e, :, 0 : n * 256],
-                y_send.at[d],
-                y_recv.at[d],
+                sent,
+                y_recv.at[Y_STAGE.index(d)],
                 (of_plane(0, e), tp),
             )
 
     def add_near(n):
-        for i in range(2):
-            drain(nr.at[i, :, :, 0 : n * 256], n_recv.at[i])
+        drain(nr.at[:, :, :, 0 : n * 256], n_recv)
         part = own_part[:, :, 0 : n * 256] + nr[0, :, :, 0 : n * 256].astype(F32) + nr[1, :, :, 0 : n * 256].astype(F32)
         own_part[:, :, 0 : n * 256] = part
         yb[0, :, :, 0 : n * 256] = part.astype(BF16)
@@ -208,23 +205,18 @@
         c = lax.rem(z + d, Z)
 
         def body(n):
-            block = pl.ds(start_of(c), n * 128)
-            gate = jnp.dot(normed, wg[:, block], preferred_element_type=F32)
-            up = jnp.dot(normed, wu[:, block], preferred_element_type=F32)
-            for i in range(n):
-                for half, value in enumerate((gate, up)):
-                    tile = value[:, i * 128 : (i + 1) * 128].reshape(Y, 8, 128)
-                    at = i * 256 + half * 128
-                    if d == 0:
-                        own_part[:, :, at : at + 128] = tile
-                    else:
-                        yb[d, :, :, at : at + 128] = tile.astype(BF16)
+            block = pl.ds(pl.multiple_of(c * 768 + jnp.maximum(c - 6, 0) * 256, 256), n * 256)
+            both = jnp.dot(normed, wgu[:, block], preferred_element_type=F32).reshape(Y, 8, n * 256)
+            if d == 0:
+                own_part[:, :, 0 : n * 256] = both
+            else:
+                yb[d, :, :, 0 : n * 256] = both.astype(BF16)
             if d in NEAR:
                 send(
                     yb.at[d, :, :, 0 : n * 256],
                     nr.at[NEAR.index(d), :, :, 0 : n * 256],
-                    y_send.at[d],
-                    n_recv.at[NEAR.index(d)],
+                    sent,
+                    n_recv,
                     (of_plane(d, 0), tp),
                 )
             elif d:
@@ -232,11 +224,10 @@
 
         by_width(c, body)
 
-    l_wg.wait()
-    l_wu.wait()
-    for d in FAR_FIRST:
+    drain(wgu, gu_sem)
+    for d in (4, 3, 5, 1, 7, 2, 6, 0):
         multiply(d)
-        if d == FAR_FIRST[1]:
+        if d == 6:
             send_squares()
 
     def finish_y(d):
@@ -244,7 +235,7 @@
 
         def body(n):
             n = n * 256
-            drain(yr.at[d, :, :, 0:n], y_recv.at[d])
+            drain(yr.at[d, :, :, 0:n], y_recv.at[Y_STAGE.index(d)])
             part = yb[d, y, :, 0:n].astype(F32) if d else own_part[y, :, 0:n]
             for i in range(Y - 1):
                 part += yr[d, i, :, 0:n].astype(F32)
@@ -252,7 +243,7 @@
                 own_sum[:, 0:n] = part
             else:
                 zs[d, :, 0:n] = part.astype(BF16)
-                send(zs.at[d, :, 0:n], zr.at[6 - d, :, 0:n], z_send.at[d], z_recv, (of_plane(d, 0), tp))
+                send(zs.at[d, :, 0:n], zr.at[6 - d, :, 0:n], sent, z_recv, (of_plane(d, 0), tp))
 
         by_width(c, body)
 
@@ -278,14 +269,11 @@
     def send_hidden(n):
         own = hr.at[z, y, :, 0 : n * 128]
         for d, e in OTHERS:
-            send(own, own, h_send, h_recv.at[(Z - d) % Z], (of_plane(d, e), tp))
+            send(own, own, sent, h_recv, (of_plane(d, e), tp))
 
     by_width(z, send_hidden)
 
-    l_wd.wait()
-    for d in (0, 4, 3, 5, 2, 6, 1, 7):
-        c = lax.rem(z + d, Z)
-        by_width(c, lambda n, c=c, d=d: drain(hr.at[c, 0 : Y - (d == 0), :, 0 : n * 128], h_recv.at[d]))
+    by_width(z, lambda n: drain(sized.at[0 : (Y * sum(WIDTH) - n) * 4], h_recv))
     hidden = jnp.concatenate(
         [hr[c, :, :, 0 : WIDTH[c] * 128].astype(F32).reshape(KV, WIDTH[c] * 128).astype(BF16) for c in range(Z)], axis=1
     )
@@ -294,7 +282,7 @@
 
     for i in FAR_FIRST[:-1]:
         to = lax.rem(tp + i, TP)
-        send(fs.at[to // 2], fr.at[TP - 1 - i], f_send, f_recv, (kv, to))
+        send(fs.at[to // 2], fr.at[TP - 1 - i], sent, f_recv, (kv, to))
 
     rows = aft[pl.ds(pl.multiple_of(x * 8, 8), 8), :] + fs[x].astype(F32)
     drain(fr, f_recv)
@@ -302,21 +290,11 @@
         rows += fr[i].astype(F32)
     layer_out[...] = jnp.where(core == 0, rows[0:4], rows[4:8]).astype(BF16)
 
-    drain(rs.at[0 : KV - 1], a_send.at[0])
-    drain(ra, a_send.at[1])
-    drain(gb.at[0 : KV - 1], b_send)
-    drain(pr.at[0 : TP - 1], c_send)
-    drain(sq.at[0 : KV - 1], sq_send)
-    for d in range(Z):
-
-        def left(n, d=d):
-            drain(yb.at[d, 0 : Y - (d not in NEAR), :, 0 : n * 256], y_send.at[d])
-            if d and d not in NEAR:
-                drain(zs.at[d, :, 0 : n * 256], z_send.at[d])
-
-        by_width(lax.rem(z + d, Z), left)
-    by_width(z, lambda n: drain(hsent.at[:, :, 0 : n * 128], h_send))
-    drain(fr, f_send)
+    def left(n):
+        units = (KV - 1) * (1 + 8 + 8 + 1 + 4 * n) + (TP - 1) * (64 + 16) + (Y * sum(WIDTH) - n) * 8
+        drain(sized.at[0:units], sent)
+
+    by_width(z, left)
 
 
 def write_out(after_in, layer_in, after_out, layer_out, sem):
@@ -350,8 +328,7 @@
             pltpu.VMEM((KV, COLS), BF16),
             pltpu.VMEM((HEADS * HD, COLS), BF16),
             pltpu.VMEM((4, 128), BF16),
-            pltpu.VMEM((COLS, FF), BF16),
-            pltpu.VMEM((COLS, FF), BF16),
+            pltpu.VMEM((COLS, 2 * FF), BF16),
             pltpu.VMEM((FF, COLS), BF16),
             pltpu.VMEM((KV, HEADS, HD), BF16),
             pltpu.VMEM((SEQS, 1, 128), F32),
@@ -371,11 +348,10 @@
             pltpu.VMEM((Z, 8, 1024), BF16),
             pltpu.VMEM((Z - 3, 8, 1024), BF16),
             pltpu.VMEM((Z, Y, 8, 512), BF16),
-            pltpu.VMEM((KV - 1, 8, 512), BF16),
+            pltpu.VMEM((2414, 1, 128), F32),
             pltpu.VMEM((4, 8, COLS), BF16),
             pltpu.VMEM((TP - 1, 8, COLS), BF16),
-            dma((12,)), dma((2,)), dma((2,)), dma, dma, dma, dma,
-            dma, dma, dma((Z,)), dma((Z,)), dma((2,)), dma((Z,)), dma, dma, dma((Z,)), dma, dma,
+            dma((7,)), dma, dma, dma((2,)), dma, dma, dma, dma((len(Y_STAGE),)), dma, dma, dma, dma,
         ],
         compiler_params=pltpu.CompilerParams(
             collective_id=0, has_side_effects=True, vmem_limit_bytes=60 * 1024 * 1024

time: 52.5 us -> 51.6 us (0.983)
  Pallas kernels: 51.7 us -> 50.8 us
    pallas_call x1, Pallas kernels: 51.1 us -> 50.2 us  [local(): pl.pallas_call(kernel, out_shape=(pltpu.VMEM((KV, COLS), BF16), pltpu.VME...]
where the time goes in v5:
time: 51.6 us; the launch traced here: 51.5 us
  Pallas kernels  50.8 us (98%)
  between operations  0.64 us (1%)
    pallas_call x1, Pallas kernels, local(): pl.pallas_call(kernel, out_shape=(pltpu.VMEM((KV, COLS), BF16), pltpu.VME...  50.2 us

profile of v5, /device:TPU:1, one launch (start us, length us, event | category | flops | bytes accessed | tf_op | source)
XLA Modules:
  0.0 51.5 jit_solution(17224043716568391391)
XLA Ops:
  0.6 50.2 %shard_map.131 = (bf16[32,512]{1,0:T(8,128)(2,1)S(1)}, bf16[4,512]{1,0:T(4,128)(2,1)S(1)}) custom-call(s32[8]{0:T(128)} %lengths_in.1, bf16[32,16,128]{2,1,0:T(8,128)(2,1)} %bitcast.8, bf16[8,256,128]{2,1,0:T(8,128)(2,1)} %bitcast.6, bf16[8,256,128]{2,1,0:T(8,128)(2,1)} %bitcast.7, bf16[8,4,128]{2,1,0:T(4,128)(2,1)} %bitcast.9, bf16[8,4,128]{2,1,0:T(4,128)(2,1)} %bitcast.10, ...), custom_call_target="tpu_custom_call" | custom-call | tf_op jit(solution)/shard_map/pallas_call | solution.py:316
  50.8 0.6 %shard_map.132 = (bf16[32,512]{1,0:T(8,128)(2,1)}, bf16[4,512]{1,0:T(4,128)(2,1)}) custom-call(bf16[32,512]{1,0:T(8,128)(2,1)S(1)} %get-tuple-element.4.after_in, bf16[4,512]{1,0:T(4,128)(2,1)S(1)} %get-tuple-element.5.layer_in), custom_call_target="tpu_custom_call" | custom-call | tf_op jit(solution)/shard_map/pallas_call | solution.py:378

commit v6 on v5

--- a/solution.py
+++ b/solution.py
@@ -278,20 +278,21 @@
         [hr[c, :, :, 0 : WIDTH[c] * 128].astype(F32).reshape(KV, WIDTH[c] * 128).astype(BF16) for c in range(Z)], axis=1
     )
     down = jnp.dot(hidden, wd[...], preferred_element_type=F32)
-    fs[...] = down.reshape(4, 8, COLS).astype(BF16)
+    fs[...] = down.reshape(TP, 4, COLS).astype(BF16)
 
     for i in FAR_FIRST[:-1]:
         to = lax.rem(tp + i, TP)
-        send(fs.at[to // 2], fr.at[TP - 1 - i], sent, f_recv, (kv, to))
-
-    rows = aft[pl.ds(pl.multiple_of(x * 8, 8), 8), :] + fs[x].astype(F32)
+        send(fs.at[to], fr.at[TP - 1 - i], sent, f_recv, (kv, to))
+
+    wide = aft[pl.ds(pl.multiple_of(x * 8, 8), 8), :]
+    rows = jnp.where(core == 0, wide[0:4], wide[4:8]) + fs[tp].astype(F32)
     drain(fr, f_recv)
     for i in range(TP - 1):
         rows += fr[i].astype(F32)
-    layer_out[...] = jnp.where(core == 0, rows[0:4], rows[4:8]).astype(BF16)
+    layer_out[...] = rows.astype(BF16)
 
     def left(n):
-        units = (KV - 1) * (1 + 8 + 8 + 1 + 4 * n) + (TP - 1) * (64 + 16) + (Y * sum(WIDTH) - n) * 8
+        units = (KV - 1) * (1 + 8 + 8 + 1 + 4 * n) + (TP - 1) * (64 + 8) + (Y * sum(WIDTH) - n) * 8
         drain(sized.at[0:units], sent)
 
     by_width(z, left)
@@ -349,8 +350,8 @@
             pltpu.VMEM((Z - 3, 8, 1024), BF16),
             pltpu.VMEM((Z, Y, 8, 512), BF16),
             pltpu.VMEM((2414, 1, 128), F32),
-            pltpu.VMEM((4, 8, COLS), BF16),
-            pltpu.VMEM((TP - 1, 8, COLS), BF16),
+            pltpu.VMEM((TP, 4, COLS), BF16),
+            pltpu.VMEM((TP - 1, 4, COLS), BF16),
             dma((7,)), dma, dma, dma((2,)), dma, dma, dma, dma((len(Y_STAGE),)), dma, dma, dma, dma,
         ],
         compiler_params=pltpu.CompilerParams(

time: 51.6 us -> 51.5 us (level)
  no operation moved by 1% of the time
where the time goes in v6:
time: 51.5 us; the launch traced here: 51.4 us
  Pallas kernels  50.8 us (99%)
  between operations  0.64 us (1%)
    pallas_call x1, Pallas kernels, local(): pl.pallas_call(kernel, out_shape=(pltpu.VMEM((KV, COLS), BF16), pltpu.VME...  50.1 us

profile of v6, /device:TPU:1, one launch (start us, length us, event | category | flops | bytes accessed | tf_op | source)
XLA Modules:
  0.0 51.4 jit_solution(6524995220631795521)
XLA Ops:
  0.6 50.1 %shard_map.131 = (bf16[32,512]{1,0:T(8,128)(2,1)S(1)}, bf16[4,512]{1,0:T(4,128)(2,1)S(1)}) custom-call(s32[8]{0:T(128)} %lengths_in.1, bf16[32,16,128]{2,1,0:T(8,128)(2,1)} %bitcast.8, bf16[8,256,128]{2,1,0:T(8,128)(2,1)} %bitcast.6, bf16[8,256,128]{2,1,0:T(8,128)(2,1)} %bitcast.7, bf16[8,4,128]{2,1,0:T(4,128)(2,1)} %bitcast.9, bf16[8,4,128]{2,1,0:T(4,128)(2,1)} %bitcast.10, ...), custom_call_target="tpu_custom_call" | custom-call | tf_op jit(solution)/shard_map/pallas_call | solution.py:317
  50.8 0.6 %shard_map.132 = (bf16[32,512]{1,0:T(8,128)(2,1)}, bf16[4,512]{1,0:T(4,128)(2,1)}) custom-call(bf16[32,512]{1,0:T(8,128)(2,1)S(1)} %get-tuple-element.4.after_in, bf16[4,512]{1,0:T(4,128)(2,1)S(1)} %get-tuple-element.5.layer_in), custom_call_target="tpu_custom_call" | custom-call | tf_op jit(solution)/shard_map/pallas_call | solution.py:379
